TPU v7x, 256 devices: a whole 4x4x8 slice. The times are simulated.
256 devices in a mesh: region: 16 (over y, x_hi, core), member: 16 (over x_lo, z).
Axes of the slice: x: 4 (x_hi: 2, x_lo: 2; x = x_hi * 2 + x_lo), y: 4, z: 8, core: 2. Of those that a mesh axis runs over, the one named last changes fastest.
Arguments:
- prior_states: float32 [32, 256, 16, 2048], P('region', 'member'), may hold values from -6 to 6
- prior_in_sensor_space: float32 [32, 256, 256], P('region', 'member'), may hold values from -10 to 10
- sensor_readings: float32 [32, 256], replicated, may hold values from -8 to 8
- error_precisions: float32 [32, 256], replicated, may hold values from 0.25 to 4
- live_tallies: int32 [32], replicated, may hold values from 1 to 256
- adjacent_areas: int32 [32, 4], replicated, may hold values from 0 to 31, as said below
- taper_lookup: int32 [32, 5, 256], replicated, may hold values from 0 to 15
- blend_lookup: int32 [32, 16, 5], P('region', 'member'), may hold values from 0 to 15
- taper_factors: float32 [16], replicated, may hold values from 0.05 to 1
Outputs:
- analysis: float32 [32, 256, 16, 2048], P('region', 'member')
Inputs may be any that keep to these rules, and one draw needn't show every extreme that they name: `adjacent_areas`: the 4 neighbours of region r are distinct, differ from r, and each neighbour q satisfies (q // 2 - r // 2) equal to -1, 0 or 1 modulo 32 // 2.
All inputs are finite; a program needn't handle non-finite values.
Results may differ from a plain program's by a relative error of at most 0.0003.
Values sent between devices are 32-bit elements; how exact they have to be, the bound alone decides.
No kernel may reach another device: no remote copies, remote signals or barrier semaphores. Data moves between devices by JAX's collectives and lax.ppermute only.
A program may use at most 64 MiB of HBM per device.

v0:
```python
import jax
import jax.numpy as jnp
from jax import lax
from jax.sharding import PartitionSpec as P

MEMBER_TOTAL = 256
NOBS = 256
NSIT = 8
REG_DEV = 2


inflation = 1.1
highest = lax.Precision.HIGHEST


def copy_for_each(array, axis):
    peers = lax.axis_size(axis)
    return lax.all_to_all(
        jnp.broadcast_to(array[None], (peers, *array.shape)), axis, 0, 0, tiled=True
    )


def joined_along(pieces, dim):
    shape = list(pieces.shape[1:])
    shape[dim] *= pieces.shape[0]
    return jnp.moveaxis(pieces, 0, dim).reshape(shape)


def gather_directly(array, axis, dim):
    pieces = copy_for_each(array, axis)
    return joined_along(pieces, dim)


def extended(cells, sides, width):
    for axis, dim in sides:
        count = lax.axis_size(axis)
        head = lax.slice_in_dim(cells, 0, width, axis=dim)
        tail = lax.slice_in_dim(cells, cells.shape[dim] - width, cells.shape[dim], axis=dim)
        cells = jnp.concatenate(
            [
                lax.ppermute(tail, axis, [(i, (i + 1) % count) for i in range(count)]),
                cells,
                lax.ppermute(head, axis, [((i + 1) % count, i) for i in range(count)]),
            ],
            axis=dim,
        )
    return cells


def split_up(array, dim, peers):
    shape = array.shape
    pieces = array.reshape(*shape[:dim], peers, shape[dim] // peers, *shape[dim + 1 :])
    return jnp.moveaxis(pieces, dim, 0)


def cut_rows(length, count):
    turn = length // count
    if turn >= 8:
        turn -= turn % 8
    return [turn * k for k in range(1, count)]


def exchange_in_pieces(array, axis, pieces, split_dim, concat_dim):
    blocks = split_up(array, split_dim, lax.axis_size(axis))
    widest = max(range(1, max(2, blocks.ndim - 1)), key=lambda d: blocks.shape[d])
    outs = []
    for piece in jnp.split(blocks, cut_rows(blocks.shape[widest], pieces), axis=widest):
        if piece.size:
            outs.append(lax.all_to_all(piece, axis, split_axis=0, concat_axis=0, tiled=True))
    return joined_along(jnp.concatenate(outs, axis=widest), concat_dim)


def newton_root(gram_mat):
    order = gram_mat.shape[-1]
    identity = jnp.eye(order, dtype=jnp.float32)
    norm_value = jnp.sqrt(jnp.sum(gram_mat * gram_mat, axis=(-2, -1)))
    scaled = gram_mat / norm_value[..., None, None]
    root_mat = jnp.broadcast_to(identity, gram_mat.shape)
    for sweep in range(NSIT):
        correction = 1.5 * identity - 0.5 * jnp.einsum(
            "...ij,...jk->...ik", root_mat, scaled, precision=highest
        )
        root_mat = jnp.einsum("...ij,...jk->...ik", correction, root_mat, precision=highest)
        if sweep + 1 < NSIT:
            scaled = jnp.einsum("...ij,...jk->...ik", scaled, correction, precision=highest)
    return (root_mat, norm_value)


def transform_of(gram_mat, drive_vec):
    members = gram_mat.shape[-1]
    root_mat, norm_value = newton_root(gram_mat)
    half_way = jnp.einsum("...jk,...k->...j", root_mat, drive_vec, precision=highest)
    mean_shift = (
        jnp.einsum("...jk,...k->...j", root_mat, half_way, precision=highest)
        / norm_value[..., None]
    )
    factor = jnp.sqrt(members - 1.0) / jnp.sqrt(norm_value)
    return factor[..., None, None] * root_mat + mean_shift[..., None]


def body(
    prior_states,
    prior_in_sensor_space,
    sensor_readings,
    error_precisions,
    live_tallies,
    adjacent_areas,
    taper_lookup,
    blend_lookup,
    taper_factors,
):
    area_sorted = lax.all_to_all(prior_states, "member", split_axis=2, concat_axis=1, tiled=True)
    region_pos = lax.axis_index("region")
    cycle_size = lax.axis_size("region")
    local_nbr = lax.dynamic_slice_in_dim(adjacent_areas, region_pos * REG_DEV, REG_DEV, 0)
    nbr_slot = (local_nbr // REG_DEV - region_pos + 1) % cycle_size * REG_DEV + local_nbr % REG_DEV
    own_slot = REG_DEV + jnp.arange(REG_DEV, dtype=jnp.int32)
    slot_table = jnp.concatenate([own_slot[:, None], nbr_slot], axis=1)
    slot_ids = jnp.arange(3 * REG_DEV, dtype=jnp.int32)
    candidate = (region_pos - 1 + slot_ids // REG_DEV) % cycle_size * REG_DEV + slot_ids % REG_DEV
    whole = gather_directly(prior_in_sensor_space, "member", 1)
    columns = extended(whole, (("region", 0),), REG_DEV)
    live_mask = (jnp.arange(NOBS, dtype=jnp.int32)[None, :] < live_tallies[:, None]).astype(
        jnp.float32
    )
    obs_weight = error_precisions * live_mask
    weight_cand = jnp.take(obs_weight, candidate, axis=0)
    value_cand = jnp.take(sensor_readings, candidate, axis=0)
    local_loc = lax.dynamic_slice_in_dim(taper_lookup, region_pos * REG_DEV, REG_DEV, 0)
    loc_weight = jnp.take(taper_factors, local_loc, axis=0)
    ens_mean = jnp.mean(columns, axis=1)
    perturb = columns - ens_mean[:, None, :]
    innovation = value_cand - ens_mean
    pert_sel = jnp.take(perturb, slot_table, axis=0)
    weight_sel = jnp.take(weight_cand, slot_table, axis=0) * loc_weight
    innov_sel = jnp.take(innovation, slot_table, axis=0)
    weighted = pert_sel * weight_sel[:, :, None, :]
    gram_part = jnp.einsum("rbkm,rbjm->rkj", weighted, pert_sel, precision=highest)
    drive_part = jnp.einsum("rbkm,rbm->rk", weighted, innov_sel, precision=highest)
    identity = jnp.eye(MEMBER_TOTAL, dtype=jnp.float32)
    gram_mat = gram_part + (MEMBER_TOTAL - 1) / inflation * identity
    transforms = transform_of(gram_mat, drive_part)
    nearby = extended(transforms, (("region", 0),), REG_DEV)
    picked = jnp.take(nearby, slot_table, axis=0)
    blend_weight = jnp.take(taper_factors, blend_lookup, axis=0)
    blend_weight = blend_weight / jnp.sum(blend_weight, axis=-1, keepdims=True)
    patch_transform = jnp.einsum("rqb,rbjk->rqjk", blend_weight, picked, precision=highest)
    center = jnp.mean(area_sorted, axis=1, keepdims=True)
    updated = center + jnp.einsum(
        "rqjk,rjqv->rkqv", patch_transform, area_sorted - center, precision=highest
    )
    return exchange_in_pieces(updated, "member", 2, 1, 2)


def solution(mesh):
    placed = (
        P("region", "member", None, None),
        P("region", "member", None),
        P(),
        P(),
        P(),
        P(),
        P(),
        P("region", "member", None),
        P(),
    )
    return jax.shard_map(
        body,
        mesh=mesh,
        in_specs=placed,
        out_specs=P("region", "member", None, None),
        check_vma=False,
    )
```

profile of v0, /device:TPU:46, one launch (start us, length us, event | category | flops | bytes accessed | tf_op | source)
XLA Modules:
  0.0 271.8 jit_solution(7934040425921623184)
XLA Ops:
  0.0 1.7 broadcast_in_dim.45
  1.7 9.5 %all-to-all-start.1 = ((f32[16,2,16,256]{3,2,1,0:T(8,128)}), f32[16,2,16,256]{3,2,1,0:T(8,128)S(1)}, u32[]{:S(2)}, u32[]{:S(2)}) async-start(f32[16,2,16,256]{3,2,1,0:T(8,128)} %broadcast_in_dim.45), calls=%async_computation.1 | async-start | bytes 1048576 | tf_op jit(solution)/shard_map/all_to_all | solution.py:18
  12.4 14.7 %gather_fusion.1 = f32[2560]{0:T(1024)S(1)} fusion(f32[16]{0:T(128)S(1)} %copy-done.2, s32[3072]{0:T(1024)S(1)} %pad_clamp_fusion), kind=kCustom, calls=%fused_computation.7 | custom fusion | bytes 30720 | tf_op jit(solution)/shard_map/jit(_take)/gather | solution.py:130
  28.3 6.6 %copy.37 = f32[2,16,16,2048]{3,1,0,2:T(8,128)} copy(f32[2,16,16,2048]{3,2,1,0:T(8,128)} %param.15) | data formatting | bytes 8388608 | tf_op args[0]
  35.0 8.1 %all-to-all-start = ((f32[2,16,16,2048]{3,1,0,2:T(8,128)}), f32[2,16,16,2048]{3,1,0,2:T(8,128)}, u32[]{:S(2)}, u32[]{:S(2)}) async-start(f32[2,16,16,2048]{3,1,0,2:T(8,128)} %copy.37), calls=%async_computation | async-start | bytes 8388608 | tf_op jit(solution)/shard_map/all_to_all | solution.py:112
  43.2 1.0 collective-permute-start
  45.0 25.1 %collective-permute-done.1 = f32[2,256,256]{2,1,0:T(8,128)S(1)} collective-permute-done((f32[2,256,256]{2,1,0:T(8,128)S(1)}, f32[2,256,256]{2,1,0:T(8,128)S(1)}, u32[]{:S(2)}, u32[]{:S(2)}) %collective-permute-start.1) | collective-permute-done | bytes 524320 | tf_op jit(solution)/shard_map/ppermute | solution.py:43
  71.7 1.3 fusion.32
  73.0 2.1 gather_fusion.2
  75.2 2.5 fusion.2
  77.7 3.0 %multiply_reduce_fusion = (f32[2]{0:T(128)S(1)}, f32[2,256,256]{2,1,0:T(8,128)S(1)}) fusion(f32[256,256]{1,0:T(8,128)S(1)} %fusion.40, f32[2,5,256,256]{3,2,1,0:T(8,128)S(1)} %bitcast.102, pred[2,5]{1,0:T(4,128)(4,1)S(1)} %copy.42, f32[2,5,256]{2,1,0:T(8,128)S(1)} %get-tuple-element.15), kind=kOutput, calls=%fused_computation.52 | convolution fusion | flops 2015625216 | bytes 3418130 | tf_op jit(solution)/shard_map/rbkm,rbjm->rkj/dot_general | solution.py:138
  87.4 0.8 fusion.67
  97.6 3.7 %collective-permute-start.3 = (f32[2,256,256]{2,1,0:T(8,128)S(1)}, f32[2,256,256]{2,1,0:T(8,128)S(1)}, u32[]{:S(2)}, u32[]{:S(2)}) collective-permute-start(f32[2,256,256]{2,1,0:T(8,128)S(1)} %multiply_add_fusion), channel_id=1, source_target_pairs={{16,0},{32,16},{48,32},{64,48},{80,64},{96,80},{112,96},{128,112},... | collective-permute-start | bytes 1572872 | tf_op jit(solution)/shard_map/ppermute | solution.py:43
  102.5 23.5 %collective-permute-done.3 = f32[2,256,256]{2,1,0:T(8,128)S(1)} collective-permute-done((f32[2,256,256]{2,1,0:T(8,128)S(1)}, f32[2,256,256]{2,1,0:T(8,128)S(1)}, u32[]{:S(2)}, u32[]{:S(2)}) %collective-permute-start.3) | collective-permute-done | bytes 524320 | tf_op jit(solution)/shard_map/ppermute | solution.py:43
  126.0 1.9 collective-permute-done.2
  128.1 2.3 gather_fusion.7
  130.3 2.1 broadcast_select_fusion
  132.4 5.2 %fusion = f32[2,1,256,256]{3,1,2,0:T(1,128)S(1)} fusion(f32[2,5,1,1]{1,2,3,0:T(1,128)S(1)} %bitcast.115, f32[2,5,256,256]{3,2,1,0:T(8,128)S(1)} %broadcast_select_fusion), kind=kOutput, calls=%fused_computation.12 | convolution fusion | flops 7864320 | bytes 3145768 | tf_op jit(solution)/shard_map/rqb,rbjk->rqjk/dot_general | solution.py:147
  138.0 2.4 bitcast_reduce_fusion
  140.4 2.5 copy.38
  143.3 4.0 %bitcast_add_fusion = f32[2,1,2048,256]{2,3,0,1:T(8,128)S(1)} fusion(f32[2,256,2048]{2,1,0:T(8,128)S(1)} %bitcast_subtract_fusion, f32[2,2048]{1,0:T(2,128)S(1)} %broadcast_multiply_fusion, f32[2,1,256,256]{2,3,0,1:T(8,128)S(1)} %copy.63), kind=kOutput, calls=%fused_computation.10 | convolution fusion | flops 3222274048 | bytes 8929280 | tf_op jit(solution)/shard_map/rqjk,rjqv->rkqv/dot_general | solution.py:149
  148.2 64.4 %all_to_all.33 = f32[16,2,8,1,2048]{4,2,1,3,0:T(8,128)S(1)} all-to-all(f32[16,2,8,1,2048]{4,2,1,3,0:T(8,128)S(1)} %get-tuple-element.6), channel_id=1, replica_groups=mesh['region'=16,'member'=16] {'member'}, dimensions={0} | all-to-all | bytes 4194304 | tf_op jit(solution)/shard_map/all_to_all | solution.py:69
  212.6 54.0 %all_to_all.34 = f32[16,2,8,1,2048]{4,2,1,3,0:T(8,128)S(1)} all-to-all(f32[16,2,8,1,2048]{4,2,1,3,0:T(8,128)S(1)} %get-tuple-element.8), channel_id=1, replica_groups=mesh['region'=16,'member'=16] {'member'}, dimensions={0} | all-to-all | bytes 4194304 | tf_op jit(solution)/shard_map/all_to_all | solution.py:69
  267.1 4.4 %copy.53 = f32[2,16,16,2048]{3,2,1,0:T(8,128)} copy(f32[2,16,16,2048]{3,1,0,2:T(8,128)S(1)} %maximum_bitcast_fusion) | data formatting | bytes 8388608 | tf_op jit(solution)/shard_map/reshape | solution.py:26
  (94 shorter events, 24.3 us)
Async XLA Ops:
  0.0 12.3 %copy-start = (s32[32,5,256]{2,0,1:T(8,128)S(1)}, s32[32,5,256]{2,0,1:T(8,128)}, u32[]{:S(2)}) copy-start(s32[32,5,256]{2,0,1:T(8,128)} %param.21) | copy-start | bytes 491524
  0.0 12.3 %copy-start.2 = (f32[16]{0:T(128)S(1)}, f32[16]{0:T(128)}, u32[]{:S(2)}) copy-start(f32[16]{0:T(128)} %param.23) | copy-start | bytes 196
  1.7 33.3 %all-to-all-start.1 = ((f32[16,2,16,256]{3,2,1,0:T(8,128)}), f32[16,2,16,256]{3,2,1,0:T(8,128)S(1)}, u32[]{:S(2)}, u32[]{:S(2)}) async-start(f32[16,2,16,256]{3,2,1,0:T(8,128)} %broadcast_in_dim.45), calls=%async_computation.1 | async-start | bytes 1048576 | tf_op jit(solution)/shard_map/all_to_all | solution.py:18
  12.3 14.8 %copy-start.4 = (f32[32,256]{1,0:T(8,128)S(1)}, f32[32,256]{1,0:T(8,128)}, u32[]{:S(2)}) copy-start(f32[32,256]{1,0:T(8,128)} %param.17) | copy-start | bytes 98308
  12.3 15.4 %copy-start.5 = (f32[32,256]{1,0:T(8,128)S(1)}, f32[32,256]{1,0:T(8,128)}, u32[]{:S(2)}) copy-start(f32[32,256]{1,0:T(8,128)} %param.18) | copy-start | bytes 98308
  12.3 15.4 %copy-start.7 = (s32[32]{0:T(128)S(1)}, s32[32]{0:T(128)}, u32[]{:S(2)}) copy-start(s32[32]{0:T(128)} %param.19) | copy-start | bytes 388
  35.0 103.0 %all-to-all-start = ((f32[2,16,16,2048]{3,1,0,2:T(8,128)}), f32[2,16,16,2048]{3,1,0,2:T(8,128)}, u32[]{:S(2)}, u32[]{:S(2)}) async-start(f32[2,16,16,2048]{3,1,0,2:T(8,128)} %copy.37), calls=%async_computation | async-start | bytes 8388608 | tf_op jit(solution)/shard_map/all_to_all | solution.py:112
  43.1 27.0 %collective-permute-start.1 = (f32[2,256,256]{2,1,0:T(8,128)S(1)}, f32[2,256,256]{2,1,0:T(8,128)S(1)}, u32[]{:S(2)}, u32[]{:S(2)}) collective-permute-start(f32[2,256,256]{2,1,0:T(8,128)S(1)} %bitcast.106), channel_id=1, source_target_pairs={{16,0},{32,16},{48,32},{64,48},{80,64},{96,80},{112,96},{128,112},... | collective-permute-start | bytes 1572872 | tf_op jit(solution)/shard_map/ppermute | solution.py:43
  43.2 27.1 %collective-permute-start = (f32[2,256,256]{2,1,0:T(8,128)S(1)}, f32[2,256,256]{2,1,0:T(8,128)S(1)}, u32[]{:S(2)}, u32[]{:S(2)}) collective-permute-start(f32[2,256,256]{2,1,0:T(8,128)S(1)} %bitcast.107), channel_id=1, source_target_pairs={{0,16},{16,32},{32,48},{48,64},{64,80},{80,96},{96,112},{112,128},... | collective-permute-start | bytes 1572872 | tf_op jit(solution)/shard_map/ppermute | solution.py:41
  77.7 3.0 %copy-start.3 = (f32[256,256]{1,0:T(8,128)S(1)}, f32[256,256]{1,0:T(8,128)}, u32[]{:S(2)}) copy-start(f32[256,256]{1,0:T(8,128)} %fusion.38) | copy-start | bytes 786436
  94.9 6.6 %copy-start.6 = (s32[2,1,5]{2,1,0:T(1,128)S(1)}, s32[2,1,5]{2,1,0:T(1,128)}, u32[]{:S(2)}) copy-start(s32[2,1,5]{2,1,0:T(1,128)} %param.22) | copy-start | bytes 124
  97.6 28.4 %collective-permute-start.3 = (f32[2,256,256]{2,1,0:T(8,128)S(1)}, f32[2,256,256]{2,1,0:T(8,128)S(1)}, u32[]{:S(2)}, u32[]{:S(2)}) collective-permute-start(f32[2,256,256]{2,1,0:T(8,128)S(1)} %multiply_add_fusion), channel_id=1, source_target_pairs={{16,0},{32,16},{48,32},{64,48},{80,64},{96,80},{112,96},{128,112},... | collective-permute-start | bytes 1572872 | tf_op jit(solution)/shard_map/ppermute | solution.py:43
  101.3 26.6 %collective-permute-start.2 = (f32[2,256,256]{2,1,0:T(8,128)S(1)}, f32[2,256,256]{2,1,0:T(8,128)S(1)}, u32[]{:S(2)}, u32[]{:S(2)}) collective-permute-start(f32[2,256,256]{2,1,0:T(8,128)S(1)} %multiply_add_fusion), channel_id=1, source_target_pairs={{0,16},{16,32},{32,48},{48,64},{64,80},{80,96},{96,112},{112,128},... | collective-permute-start | bytes 1572872 | tf_op jit(solution)/shard_map/ppermute | solution.py:41
  266.6 4.9 %copy-start.1 = (s32[32,5,256]{2,0,1:T(8,128)S(1)}, s32[32,5,256]{2,0,1:T(8,128)}, u32[]{:S(2)}) copy-start(s32[32,5,256]{2,0,1:T(8,128)} %param.21) | copy-start | bytes 491524
where the time goes:
time: 277 us; the launch traced here: 272 us
  blocking collectives  118 us (43%)
  waiting for transfers between devices  50.7 us (18%)
  local copies, waits for them, and re-layouts  39 us (14%)
  matrix products  31.1 us (11%)
  starting transfers between devices  22.6 us (8%)
  other arithmetic  9.29 us (3%)
    all_to_all x2, blocking collectives, exchange_in_pieces(): lax.all_to_all(piece, axis, split_axis=0, concat_axis=0, tiled=True)  118 us
    ppermute x2, waiting for transfers between devices, extended(): lax.ppermute(head, axis, [((i + 1) % count, i) for i in range(count)])  48.6 us
    gather x2, local copies, waits for them, and re-layouts, body(): loc_weight = jnp.take(taper_factors, local_loc, axis=0)  14.7 us
    all_to_all x1, starting transfers between devices, copy_for_each(): lax.all_to_all(jnp.broadcast_to(array[None], (peers, *array.shape)), axis...  9.49 us
    all_to_all x1, starting transfers between devices, body(): lax.all_to_all(prior_states, 'member', split_axis=2, concat_axis=1, tiled...  8.13 us
    unnamed x17, local copies, waits for them, and re-layouts  6.67 us
  transfers between devices with their start and end apart: 6, of which 4 were waited for; matrix products, arithmetic and copies ran while one was open for 23% of the time, Pallas kernels for 0%

commit v1 on v0

v1 whole, which is shorter than its diff:
```python
import jax
import jax.numpy as jnp
from jax import lax
from jax.sharding import PartitionSpec as P

MEMBER_TOTAL = 256
NOBS = 256
NSIT = 8
REG_DEV = 2
LEVELS = 16

inflation = 1.1
highest = lax.Precision.HIGHEST


def table_lookup(table, index):
    out = jnp.zeros(index.shape, table.dtype)
    for level in range(LEVELS):
        out = jnp.where(index == level, table[level], out)
    return out


def gather_members(array, dim):
    peers = lax.axis_size("member")
    pieces = lax.all_to_all(
        jnp.broadcast_to(array[None], (peers, *array.shape)), "member", 0, 0, tiled=True
    )
    shape = list(array.shape)
    shape[dim] *= peers
    return jnp.moveaxis(pieces, 0, dim).reshape(shape)


def extended(cells):
    count = lax.axis_size("region")
    return jnp.concatenate(
        [
            lax.ppermute(cells, "region", [(i, (i + 1) % count) for i in range(count)]),
            cells,
            lax.ppermute(cells, "region", [((i + 1) % count, i) for i in range(count)]),
        ],
        axis=0,
    )


def newton_root(gram_mat):
    order = gram_mat.shape[-1]
    identity = jnp.eye(order, dtype=jnp.float32)
    norm_value = jnp.sqrt(jnp.sum(gram_mat * gram_mat, axis=(-2, -1)))
    scaled = gram_mat / norm_value[..., None, None]
    root_mat = jnp.broadcast_to(identity, gram_mat.shape)
    for sweep in range(NSIT):
        correction = 1.5 * identity - 0.5 * jnp.einsum(
            "...ij,...jk->...ik", root_mat, scaled, precision=highest
        )
        root_mat = jnp.einsum("...ij,...jk->...ik", correction, root_mat, precision=highest)
        if sweep + 1 < NSIT:
            scaled = jnp.einsum("...ij,...jk->...ik", scaled, correction, precision=highest)
    return (root_mat, norm_value)


def transform_of(gram_mat, drive_vec):
    members = gram_mat.shape[-1]
    root_mat, norm_value = newton_root(gram_mat)
    half_way = jnp.einsum("...jk,...k->...j", root_mat, drive_vec, precision=highest)
    mean_shift = (
        jnp.einsum("...jk,...k->...j", root_mat, half_way, precision=highest)
        / norm_value[..., None]
    )
    factor = jnp.sqrt(members - 1.0) / jnp.sqrt(norm_value)
    return factor[..., None, None] * root_mat + mean_shift[..., None]


def body(
    prior_states,
    prior_in_sensor_space,
    sensor_readings,
    error_precisions,
    live_tallies,
    adjacent_areas,
    taper_lookup,
    blend_lookup,
    taper_factors,
):
    whole = gather_members(prior_in_sensor_space, 1)
    states = []
    for region in range(REG_DEV):
        by_patch = jnp.swapaxes(prior_states[region], 0, 1)
        moved = lax.all_to_all(by_patch, "member", 0, 0, tiled=True)
        states.append(moved.reshape(MEMBER_TOTAL, -1))

    region_pos = lax.axis_index("region")
    cycle_size = lax.axis_size("region")
    local_nbr = lax.dynamic_slice_in_dim(adjacent_areas, region_pos * REG_DEV, REG_DEV, 0)
    nbr_slot = (local_nbr // REG_DEV - region_pos + 1) % cycle_size * REG_DEV + local_nbr % REG_DEV
    own_slot = REG_DEV + jnp.arange(REG_DEV, dtype=jnp.int32)
    slot_table = jnp.concatenate([own_slot[:, None], nbr_slot], axis=1)
    slot_ids = jnp.arange(3 * REG_DEV, dtype=jnp.int32)
    candidate = (region_pos - 1 + slot_ids // REG_DEV) % cycle_size * REG_DEV + slot_ids % REG_DEV
    columns = extended(whole)
    live_mask = (jnp.arange(NOBS, dtype=jnp.int32)[None, :] < live_tallies[:, None]).astype(
        jnp.float32
    )
    obs_weight = error_precisions * live_mask
    weight_cand = jnp.take(obs_weight, candidate, axis=0)
    value_cand = jnp.take(sensor_readings, candidate, axis=0)
    local_loc = lax.dynamic_slice_in_dim(taper_lookup, region_pos * REG_DEV, REG_DEV, 0)
    loc_weight = table_lookup(taper_factors, local_loc)
    ens_mean = jnp.mean(columns, axis=1)
    perturb = columns - ens_mean[:, None, :]
    innovation = value_cand - ens_mean
    pert_sel = jnp.take(perturb, slot_table, axis=0)
    weight_sel = jnp.take(weight_cand, slot_table, axis=0) * loc_weight
    innov_sel = jnp.take(innovation, slot_table, axis=0)
    weighted = pert_sel * weight_sel[:, :, None, :]
    gram_part = jnp.einsum("rbkm,rbjm->rkj", weighted, pert_sel, precision=highest)
    drive_part = jnp.einsum("rbkm,rbm->rk", weighted, innov_sel, precision=highest)
    identity = jnp.eye(MEMBER_TOTAL, dtype=jnp.float32)
    gram_mat = gram_part + (MEMBER_TOTAL - 1) / inflation * identity
    transforms = transform_of(gram_mat, drive_part)
    nearby = extended(transforms)
    blend_weight = table_lookup(taper_factors, blend_lookup[:, 0])
    blend_weight = blend_weight / jnp.sum(blend_weight, axis=-1, keepdims=True)

    finished = []
    for region in range(REG_DEV):
        picked = jnp.take(nearby, slot_table[region], axis=0)
        patch_transform = jnp.sum(blend_weight[region][:, None, None] * picked, axis=0)
        center = jnp.mean(states[region], axis=0, keepdims=True)
        updated = center + jnp.einsum(
            "jk,jv->kv", patch_transform, states[region] - center, precision=highest
        )
        pieces = updated.reshape(lax.axis_size("member"), -1, updated.shape[-1])
        back = lax.all_to_all(pieces, "member", 0, 0, tiled=True)
        finished.append(jnp.swapaxes(back, 0, 1))
    return jnp.stack(finished)


def solution(mesh):
    placed = (
        P("region", "member", None, None),
        P("region", "member", None),
        P(),
        P(),
        P(),
        P(),
        P(),
        P("region", "member", None),
        P(),
    )
    return jax.shard_map(
        body,
        mesh=mesh,
        in_specs=placed,
        out_specs=P("region", "member", None, None),
        check_vma=False,
    )
```

time: 277 us -> 287 us (1.036)
  blocking collectives: 118 us -> 55.8 us
  waiting for transfers between devices: 50.7 us -> 89.9 us
  other arithmetic: 9.29 us -> 36 us
  starting transfers between devices: 22.6 us -> 39.1 us
  local copies, waits for them, and re-layouts: 39 us -> 28.5 us
    all_to_all x2 -> x1, blocking collectives: 118 us -> 55.8 us  [body(): back = lax.all_to_all(pieces, 'member', 0, 0, tiled=True)]
    all_to_all x2 -> x4, waiting for transfers between devices: 0.01 us -> 50.1 us  [the longest x1 41.4 us: body(): back = lax.all_to_all(pieces, 'member', 0, 0, tiled=True)]
    all_to_all x2 -> x4, starting transfers between devices: 17.6 us -> 36.3 us  [the longest x2 17.9 us: body(): moved = lax.all_to_all(by_patch, 'member', 0, 0, tiled=True)]
    gather x5 -> x2, local copies, waits for them, and re-layouts: 17.7 us -> 6.2 us  [body(): picked = jnp.take(nearby, slot_table[region], axis=0)]
    ppermute x4, waiting for transfers between devices: 50.7 us -> 39.7 us  [the longest x2 33.2 us: extended(): lax.ppermute(cells, 'region', [((i + 1) % count, i) for i in range(count)])]
    mul x0 -> x1, other arithmetic: none -> 9.95 us  [body(): weight_sel = jnp.take(weight_cand, slot_table, axis=0) * loc_weight]
    select_n x4 -> x3, other arithmetic: 2.08 us -> 9.34 us  [the longest x1 9.25 us: table_lookup(): out = jnp.where(index == level, table[level], out)]
    reshape x2 -> x0, local copies, waits for them, and re-layouts: 4.93 us -> none  [the longest x1 4.45 us: joined_along(): return jnp.moveaxis(pieces, 0, dim).reshape(shape)]
  transfers between devices with their start and end apart: 6 -> 8, of which waited for: 4 -> 6; matrix products, arithmetic and copies ran while one was open for 23% -> 31% of each run, Pallas kernels for 0% -> 0%
where the time goes in v1:
time: 287 us; the launch traced here: 282 us
  waiting for transfers between devices  89.9 us (31%)
  blocking collectives  55.8 us (19%)
  starting transfers between devices  39.1 us (14%)
  other arithmetic  36 us (13%)
  matrix products  31.7 us (11%)
  local copies, waits for them, and re-layouts  28.5 us (10%)
    all_to_all x1, blocking collectives, body(): back = lax.all_to_all(pieces, 'member', 0, 0, tiled=True)  55.8 us
    all_to_all x1, waiting for transfers between devices, body(): back = lax.all_to_all(pieces, 'member', 0, 0, tiled=True)  41.4 us
    ppermute x2, waiting for transfers between devices, extended(): lax.ppermute(cells, 'region', [((i + 1) % count, i) for i in range(count)])  33.2 us
    all_to_all x2, starting transfers between devices, body(): moved = lax.all_to_all(by_patch, 'member', 0, 0, tiled=True)  17.9 us
    mul x1, other arithmetic, body(): weight_sel = jnp.take(weight_cand, slot_table, axis=0) * loc_weight  9.95 us
    all_to_all x1, starting transfers between devices, gather_members(): lax.all_to_all(jnp.broadcast_to(array[None], (peers, *array.shape)), 'mem...  9.49 us
    select_n x1, other arithmetic, table_lookup(): out = jnp.where(index == level, table[level], out)  9.25 us
    all_to_all x1, starting transfers between devices, body(): back = lax.all_to_all(pieces, 'member', 0, 0, tiled=True)  8.88 us
  transfers between devices with their start and end apart: 8, of which 6 were waited for; matrix products, arithmetic and copies ran while one was open for 31% of the time, Pallas kernels for 0%

profile of v1, /device:TPU:46, one launch (start us, length us, event | category | flops | bytes accessed | tf_op | source)
XLA Modules:
  0.0 281.9 jit_solution(3637779208752413522)
XLA Ops:
  1.6 9.5 %all-to-all-start.1 = ((f32[16,2,16,256]{3,2,1,0:T(8,128)}), f32[16,2,16,256]{3,2,1,0:T(8,128)S(1)}, u32[]{:S(2)}, u32[]{:S(2)}) async-start(f32[16,2,16,256]{3,2,1,0:T(8,128)} %broadcast_in_dim.187), calls=%async_computation.1 | async-start | bytes 1048576 | tf_op jit(solution)/shard_map/all_to_all | solution.py:25
  18.0 2.5 fusion.61
  20.5 2.5 copy.122
  23.0 2.5 copy.121
  25.6 9.3 %compare_select_fusion.16 = f32[2,1,5]{2,1,0:T(1,128)S(1)} fusion(s32[2,1,5]{2,1,0:T(1,128)S(1)} %copy-done.5, f32[]{:T(128)} %bitcast.3, f32[]{:T(128)} %bitcast.4, f32[]{:T(128)} %bitcast.5, f32[]{:T(128)} %bitcast.6, f32[]{:T(128)} %bitcast.7, f32[]{:T(128)} %bitcast.8, f32[]{:T(128)} %bitcast.9, f32[]{:T(128)} %bitcast.10, f32[]{:T(128)} %bitcast.11, ...), kind=kLoop, calls=%fused_computation.114 | loop fusion | flops 300 | bytes 140 | tf_op jit(solution)/shard_map/jit(_where)/select_n | solution.py:19
  36.6 8.1 %all-to-all-start = ((f32[16,16,2048]{2,1,0:T(8,128)}), f32[16,16,2048]{2,1,0:T(8,128)}, u32[]{:S(2)}, u32[]{:S(2)}) async-start(f32[16,16,2048]{2,1,0:T(8,128)} %bitcast.121), calls=%async_computation | async-start | bytes 4194304 | tf_op jit(solution)/shard_map/all_to_all | solution.py:88
  45.5 18.6 %collective-permute-done.1 = f32[2,256,256]{2,1,0:T(8,128)S(1)} collective-permute-done((f32[2,256,256]{2,1,0:T(8,128)S(1)}, f32[2,256,256]{2,1,0:T(8,128)S(1)}, u32[]{:S(2)}, u32[]{:S(2)}) %collective-permute-start.1) | collective-permute-done | bytes 524320 | tf_op jit(solution)/shard_map/ppermute | solution.py:39
  64.1 2.2 collective-permute-done
  68.4 2.1 gather_fusion
  70.6 9.9 %select_multiply_fusion.2 = f32[2,5,256]{2,1,0:T(8,128)S(1)} fusion(f32[2,5,256]{2,1,0:T(8,128)S(1)} %reshape.294, s32[2,5,256]{2,0,1:T(2,128)S(1)} %constant_dynamic-slice_fusion, f32[]{:T(128)} %bitcast.17, f32[]{:T(128)} %bitcast.16, f32[]{:T(128)} %bitcast.15, f32[]{:T(128)} %bitcast.14, f32[]{:T(128)} %bitcast.13, f32[]{:T(128)} %bitcast.12, ...), kind=kLoop, calls=%fused_computation.82 | loop fusion | flops 87040 | bytes 30794 | tf_op jit(solution)/shard_map/mul | solution.py:112
  80.5 3.0 %multiply_reduce_fusion = (f32[2]{0:T(128)S(1)}, f32[2,256,256]{2,1,0:T(8,128)S(1)}) fusion(f32[256,256]{1,0:T(8,128)S(1)} %fusion.39, f32[2,5,256,256]{3,2,1,0:T(8,128)S(1)} %bitcast.124, pred[2,5]{1,0:T(4,128)(4,1)S(1)} %copy.35, f32[2,5,256]{2,1,0:T(8,128)S(1)} %select_multiply_fusion.2), kind=kOutput, calls=%fused_computation.53 | convolution fusion | flops 2015625216 | bytes 3418130 | tf_op jit(solution)/shard_map/rbkm,rbjm->rkj/dot_general | solution.py:115
  87.8 2.5 fusion
  102.8 9.8 %all-to-all-start.3 = ((f32[16,16,2048]{2,1,0:T(8,128)}), f32[16,16,2048]{2,1,0:T(8,128)S(1)}, u32[]{:S(2)}, u32[]{:S(2)}) async-start(f32[16,16,2048]{2,1,0:T(8,128)} %bitcast.126), calls=%async_computation.3 | async-start | bytes 4194304 | tf_op jit(solution)/shard_map/all_to_all | solution.py:88
  121.6 14.6 %collective-permute-done.3 = f32[2,256,256]{2,1,0:T(8,128)S(1)} collective-permute-done((f32[2,256,256]{2,1,0:T(8,128)S(1)}, f32[2,256,256]{2,1,0:T(8,128)S(1)}, u32[]{:S(2)}, u32[]{:S(2)}) %collective-permute-start.3) | collective-permute-done | bytes 524320 | tf_op jit(solution)/shard_map/ppermute | solution.py:39
  136.2 4.4 %collective-permute-done.2 = f32[2,256,256]{2,1,0:T(8,128)S(1)} collective-permute-done((f32[2,256,256]{2,1,0:T(8,128)S(1)}, f32[2,256,256]{2,1,0:T(8,128)S(1)}, u32[]{:S(2)}, u32[]{:S(2)}) %collective-permute-start.2) | collective-permute-done | bytes 524320 | tf_op jit(solution)/shard_map/ppermute | solution.py:37
  141.9 3.1 %gather_fusion.5 = f32[5,256,256]{2,1,0:T(8,128)} fusion(f32[6,256,256]{2,1,0:T(8,128)} %pad_maximum_fusion.2, s32[1024]{0:T(1024)S(1)} %pad_clamp_fusion.1), kind=kCustom, calls=%fused_computation.2.clone | custom fusion | bytes 2621460 | tf_op jit(solution)/shard_map/jit(_take)/gather | solution.py:126
  150.1 3.2 %convolution_add_fusion.1 = f32[256,2048]{1,0:T(8,128)} fusion(f32[256,256]{1,0:T(8,128)S(1)} %fusion.7, f32[256,2048]{1,0:T(8,128)S(1)} %bitcast_subtract_fusion.1, f32[2048]{0:T(1024)S(1)} %broadcast_multiply_fusion.2), kind=kOutput, calls=%fused_computation.13 | convolution fusion | flops 1611137024 | bytes 4464640 | tf_op jit(solution)/shard_map/jk,jv->kv/dot_general | solution.py:129
  153.3 8.7 %all-to-all-done.3 = f32[16,16,2048]{2,1,0:T(8,128)S(1)} async-done(((f32[16,16,2048]{2,1,0:T(8,128)}), f32[16,16,2048]{2,1,0:T(8,128)S(1)}, u32[]{:S(2)}, u32[]{:S(2)}) %all-to-all-start.3) | async-done | bytes 2097184 | tf_op jit(solution)/shard_map/all_to_all | solution.py:88
  162.0 8.9 %all-to-all-start.2 = ((f32[16,16,2048]{2,1,0:T(8,128)}), f32[16,16,2048]{2,1,0:T(8,128)}, u32[]{:S(2)}, u32[]{:S(2)}) async-start(f32[16,16,2048]{2,1,0:T(8,128)} %bitcast.127), calls=%async_computation.2 | async-start | bytes 4194304 | tf_op jit(solution)/shard_map/all_to_all | solution.py:133
  170.9 3.1 %gather_fusion.6 = f32[5,256,256]{2,1,0:T(8,128)} fusion(f32[6,256,256]{2,1,0:T(8,128)} %pad_maximum_fusion.2, s32[1024]{0:T(1024)S(1)} %pad_clamp_fusion), kind=kCustom, calls=%fused_computation.5.clone | custom fusion | bytes 2621460 | tf_op jit(solution)/shard_map/jit(_take)/gather | solution.py:126
  177.9 41.4 %all-to-all-done.2 = f32[16,16,2048]{2,1,0:T(8,128)} async-done(((f32[16,16,2048]{2,1,0:T(8,128)}), f32[16,16,2048]{2,1,0:T(8,128)}, u32[]{:S(2)}, u32[]{:S(2)}) %all-to-all-start.2) | async-done | bytes 2097184 | tf_op jit(solution)/shard_map/all_to_all | solution.py:133
  219.3 55.8 %all_to_all.25 = f32[16,16,2048]{2,1,0:T(8,128)S(1)} all-to-all(f32[16,16,2048]{2,1,0:T(8,128)S(1)} %bitcast.128), channel_id=1, replica_groups=mesh['region'=16,'member'=16] {'member'}, dimensions={0} | all-to-all | bytes 4194304 | tf_op jit(solution)/shard_map/all_to_all | solution.py:133
  275.1 2.0 pad_maximum_fusion
  277.1 4.4 %copy.45 = f32[2,16,16,2048]{3,2,1,0:T(8,128)} copy(f32[2,16,16,2048]{3,1,2,0:T(8,128)S(1)} %pad_maximum_fusion) | data formatting | bytes 8388608 | tf_op jit(solution)/shard_map/stack | solution.py:135
  (103 shorter events, 48.9 us)
Async XLA Ops:
  0.0 35.7 %copy-start = (s32[32,5,256]{2,0,1:T(8,128)S(1)}, s32[32,5,256]{2,0,1:T(8,128)}, u32[]{:S(2)}) copy-start(s32[32,5,256]{2,0,1:T(8,128)} %param.21) | copy-start | bytes 491524
  1.6 34.9 %all-to-all-start.1 = ((f32[16,2,16,256]{3,2,1,0:T(8,128)}), f32[16,2,16,256]{3,2,1,0:T(8,128)S(1)}, u32[]{:S(2)}, u32[]{:S(2)}) async-start(f32[16,2,16,256]{3,2,1,0:T(8,128)} %broadcast_in_dim.187), calls=%async_computation.1 | async-start | bytes 1048576 | tf_op jit(solution)/shard_map/all_to_all | solution.py:25
  23.0 2.5 copy-start.5
  36.6 66.2 %all-to-all-start = ((f32[16,16,2048]{2,1,0:T(8,128)}), f32[16,16,2048]{2,1,0:T(8,128)}, u32[]{:S(2)}, u32[]{:S(2)}) async-start(f32[16,16,2048]{2,1,0:T(8,128)} %bitcast.121), calls=%async_computation | async-start | bytes 4194304 | tf_op jit(solution)/shard_map/all_to_all | solution.py:88
  44.8 19.4 %collective-permute-start.1 = (f32[2,256,256]{2,1,0:T(8,128)S(1)}, f32[2,256,256]{2,1,0:T(8,128)S(1)}, u32[]{:S(2)}, u32[]{:S(2)}) collective-permute-start(f32[2,256,256]{2,1,0:T(8,128)S(1)} %bitcast.130), channel_id=1, source_target_pairs={{16,0},{32,16},{48,32},{64,48},{80,64},{96,80},{112,96},{128,112},... | collective-permute-start | bytes 1572872 | tf_op jit(solution)/shard_map/ppermute | solution.py:39
  44.8 21.5 %collective-permute-start = (f32[2,256,256]{2,1,0:T(8,128)S(1)}, f32[2,256,256]{2,1,0:T(8,128)S(1)}, u32[]{:S(2)}, u32[]{:S(2)}) collective-permute-start(f32[2,256,256]{2,1,0:T(8,128)S(1)} %bitcast.131), channel_id=1, source_target_pairs={{0,16},{16,32},{32,48},{48,64},{64,80},{80,96},{96,112},{112,128},... | collective-permute-start | bytes 1572872 | tf_op jit(solution)/shard_map/ppermute | solution.py:37
  80.5 3.0 %copy-start.4 = (f32[256,256]{1,0:T(8,128)S(1)}, f32[256,256]{1,0:T(8,128)}, u32[]{:S(2)}) copy-start(f32[256,256]{1,0:T(8,128)} %fusion.37) | copy-start | bytes 786436
  87.7 2.6 copy-start.2
  87.7 2.6 copy-start.3
  100.5 0.8 copy-start.1
  102.8 59.2 %all-to-all-start.3 = ((f32[16,16,2048]{2,1,0:T(8,128)}), f32[16,16,2048]{2,1,0:T(8,128)S(1)}, u32[]{:S(2)}, u32[]{:S(2)}) async-start(f32[16,16,2048]{2,1,0:T(8,128)} %bitcast.126), calls=%async_computation.3 | async-start | bytes 4194304 | tf_op jit(solution)/shard_map/all_to_all | solution.py:88
  118.8 17.5 %collective-permute-start.3 = (f32[2,256,256]{2,1,0:T(8,128)S(1)}, f32[2,256,256]{2,1,0:T(8,128)S(1)}, u32[]{:S(2)}, u32[]{:S(2)}) collective-permute-start(f32[2,256,256]{2,1,0:T(8,128)S(1)} %multiply_add_fusion), channel_id=1, source_target_pairs={{16,0},{32,16},{48,32},{64,48},{80,64},{96,80},{112,96},{128,112},... | collective-permute-start | bytes 1572872 | tf_op jit(solution)/shard_map/ppermute | solution.py:39
  120.7 19.9 %collective-permute-start.2 = (f32[2,256,256]{2,1,0:T(8,128)S(1)}, f32[2,256,256]{2,1,0:T(8,128)S(1)}, u32[]{:S(2)}, u32[]{:S(2)}) collective-permute-start(f32[2,256,256]{2,1,0:T(8,128)S(1)} %multiply_add_fusion), channel_id=1, source_target_pairs={{0,16},{16,32},{32,48},{48,64},{64,80},{80,96},{96,112},{112,128},... | collective-permute-start | bytes 1572872 | tf_op jit(solution)/shard_map/ppermute | solution.py:37
  162.0 57.3 %all-to-all-start.2 = ((f32[16,16,2048]{2,1,0:T(8,128)}), f32[16,16,2048]{2,1,0:T(8,128)}, u32[]{:S(2)}, u32[]{:S(2)}) async-start(f32[16,16,2048]{2,1,0:T(8,128)} %bitcast.127), calls=%async_computation.2 | async-start | bytes 4194304 | tf_op jit(solution)/shard_map/all_to_all | solution.py:133

commit v2 on v1

v2 whole, which is shorter than its diff:
```python
import functools

import jax
import jax.numpy as jnp
from jax import lax
from jax.experimental import pallas as pl
from jax.experimental.pallas import tpu as pltpu
from jax.sharding import PartitionSpec as P

MEMBER_TOTAL = 256
NOBS = 256
NBR = 4
NSIT = 8
REG_DEV = 2
LEVELS = 16
TILE_POINTS = 2048
SHARES = 16
SHARE = 16
RINGS = 8

inflation = 1.1
highest = lax.Precision.HIGHEST
SMEM = pl.BlockSpec(memory_space=pltpu.SMEM)


def dot(a, b):
    return lax.dot_general(
        a, b, (((1,), (0,)), ((), ())), precision=highest, preferred_element_type=jnp.float32
    )


def dot_rows(a, b):
    return lax.dot_general(
        a, b, (((1,), (1,)), ((), ())), precision=highest, preferred_element_type=jnp.float32
    )


def column_block(ref):
    width = ref.shape[-1]
    return pl.ds(pl.multiple_of(pl.program_id(0) * width, width), width)


def pack_kernel(x_ref, o_ref):
    o_ref[...] = jnp.swapaxes(x_ref[0], 0, 1)


def pack(states, region):
    width = 512
    return pl.pallas_call(
        pack_kernel,
        grid=(TILE_POINTS // width,),
        in_specs=[pl.BlockSpec((1, SHARE, SHARES, width), lambda i: (region, 0, 0, i))],
        out_specs=pl.BlockSpec((SHARES, SHARE, width), lambda i: (0, 0, i)),
        out_shape=pltpu.HBM((SHARES, SHARE, TILE_POINTS), jnp.float32),
        cost_estimate=pl.CostEstimate(flops=0, bytes_accessed=4 << 20, transcendentals=0),
        name="pack",
    )(states)


def unpack_kernel(x_ref, *refs):
    refs[-1][0] = jnp.swapaxes(x_ref[:, :, column_block(refs[-1])], 0, 1)


def unpack(pieces, region, target=None):
    width = 512
    extra = [] if target is None else [target]
    return pl.pallas_call(
        unpack_kernel,
        grid=(TILE_POINTS // width,),
        in_specs=[pl.BlockSpec(memory_space=pltpu.VMEM)]
        + [pl.BlockSpec(memory_space=pl.ANY)] * len(extra),
        out_specs=pl.BlockSpec((1, SHARE, SHARES, width), lambda i: (region, 0, 0, i)),
        out_shape=jax.ShapeDtypeStruct((REG_DEV, SHARE, SHARES, TILE_POINTS), jnp.float32),
        input_output_aliases={1: 0} if extra else {},
        cost_estimate=pl.CostEstimate(flops=0, bytes_accessed=4 << 20, transcendentals=0),
        name="unpack",
    )(pltpu.with_memory_space_constraint(pieces, pltpu.VMEM), *extra)


def slot_of(area, place, cycle):
    ring = lax.rem(area // REG_DEV - place + 1 + cycle, cycle)
    return ring * REG_DEV + lax.rem(area, REG_DEV)


def area_of(block, row, neighbours):
    return row if block == 0 else neighbours[row, block - 1]


def analysis_kernel(
    cycle,
    place_ref,
    live_ref,
    nbr_ref,
    factor_ref,
    prev_ref,
    own_ref,
    next_ref,
    values_ref,
    precision_ref,
    lookup_ref,
    out_ref,
    pert,
    mean,
    scaled,
    root,
):
    place = place_ref[0]
    for ring, source in enumerate((prev_ref, own_ref, next_ref)):
        for part in range(REG_DEV):
            block = source[:, part].reshape(MEMBER_TOTAL, NOBS)
            average = jnp.sum(block, axis=0, keepdims=True) * (1.0 / MEMBER_TOTAL)
            pert[ring * REG_DEV + part] = block - average
            mean[ring * REG_DEV + part] = jnp.broadcast_to(average, (8, NOBS))
    slots = lax.broadcasted_iota(jnp.int32, (1, NOBS), 1)
    rows = lax.broadcasted_iota(jnp.int32, (MEMBER_TOTAL, MEMBER_TOTAL), 0)
    cols = lax.broadcasted_iota(jnp.int32, (MEMBER_TOTAL, MEMBER_TOTAL), 1)
    identity = jnp.where(rows == cols, 1.0, 0.0).astype(jnp.float32)
    drives, norms = [], []
    for region in range(REG_DEV):
        row = place * REG_DEV + region
        lookup = lookup_ref[region]
        taper = jnp.zeros(lookup.shape, jnp.float32)
        for level in range(LEVELS):
            taper = jnp.where(lookup == level, factor_ref[level], taper)
        gram = ((MEMBER_TOTAL - 1) / inflation) * identity
        drive = jnp.zeros((MEMBER_TOTAL, 128), jnp.float32)
        for block in range(NBR + 1):
            area = area_of(block, row, nbr_ref)
            slot = slot_of(area, place, cycle)
            weight = jnp.where(slots < live_ref[area], precision_ref[pl.ds(area, 1), :], 0.0)
            weight = weight * taper[block : block + 1, :]
            offset = values_ref[pl.ds(area, 1), :] - mean[slot][0:1, :]
            block_pert = pert[slot]
            gram = gram + dot_rows(block_pert * weight, block_pert)
            drive = drive + dot_rows(
                block_pert, jnp.broadcast_to(weight * offset, (128, NOBS))
            )
        norm = jnp.sqrt(jnp.sum(gram * gram, keepdims=True))
        scaled[region] = gram / norm
        root[region] = identity
        drives.append(drive)
        norms.append(norm)

    def sweep(_, carry):
        for region in range(REG_DEV):
            step = 1.5 * identity - 0.5 * dot(root[region], scaled[region])
            root[region] = dot(step, root[region])
            scaled[region] = dot(scaled[region], step)
        return carry

    lax.fori_loop(0, NSIT, sweep, 0)
    for region in range(REG_DEV):
        root_mat = root[region]
        shift = dot(root_mat, dot(root_mat, drives[region])) / norms[region]
        factor = jnp.sqrt(jnp.float32(MEMBER_TOTAL - 1)) / jnp.sqrt(norms[region])
        out_ref[region] = factor * root_mat + jnp.concatenate([shift, shift], axis=1)


def analysis(cycle, place, live, nbr, factors, prev, own, after, values, precisions, lookup):
    whole = lambda *shape: pl.BlockSpec(shape, lambda i, *_: (0,) * len(shape))
    cells = whole(SHARES, REG_DEV, SHARE, NOBS)
    areas = values.shape[0]
    return pl.pallas_call(
        functools.partial(analysis_kernel, cycle),
        grid_spec=pltpu.PrefetchScalarGridSpec(
            num_scalar_prefetch=4,
            grid=(1,),
            in_specs=[
                cells,
                cells,
                cells,
                whole(areas, NOBS),
                whole(areas, NOBS),
                pl.BlockSpec((REG_DEV, NBR + 1, NOBS), lambda i, p, *_: (p[0], 0, 0)),
            ],
            out_specs=whole(REG_DEV, MEMBER_TOTAL, MEMBER_TOTAL),
            scratch_shapes=[
                pltpu.VMEM((3 * REG_DEV, MEMBER_TOTAL, NOBS), jnp.float32),
                pltpu.VMEM((3 * REG_DEV, 8, NOBS), jnp.float32),
                pltpu.VMEM((REG_DEV, MEMBER_TOTAL, MEMBER_TOTAL), jnp.float32),
                pltpu.VMEM((REG_DEV, MEMBER_TOTAL, MEMBER_TOTAL), jnp.float32),
            ],
        ),
        out_shape=jax.ShapeDtypeStruct((REG_DEV, MEMBER_TOTAL, MEMBER_TOTAL), jnp.float32),
        compiler_params=pltpu.CompilerParams(vmem_limit_bytes=24 << 20),
        cost_estimate=pl.CostEstimate(
            flops=70 * 6 * 2 * 256**3, bytes_accessed=3 << 20, transcendentals=0
        ),
        name="analysis",
    )(place, live, nbr, factors, prev, own, after, values, precisions, lookup)


def apply_kernel(
    cycle, region, place_ref, nbr_ref, factor_ref, blend_ref, prev_ref, own_ref, next_ref, x_ref, o_ref, mix
):
    @pl.when(pl.program_id(0) == 0)
    def _():
        place = place_ref[0]
        row = place * REG_DEV + region
        shares = [jnp.float32(0.0)] * (3 * REG_DEV)
        total = jnp.float32(0.0)
        for block in range(NBR + 1):
            slot = slot_of(area_of(block, row, nbr_ref), place, cycle)
            value = factor_ref[blend_ref[region, 0, block]]
            total = total + value
            shares = [s + jnp.where(slot == k, value, 0.0) for k, s in enumerate(shares)]
        acc = jnp.zeros((MEMBER_TOTAL, MEMBER_TOTAL), jnp.float32)
        for ring, source in enumerate((prev_ref, own_ref, next_ref)):
            for part in range(REG_DEV):
                acc = acc + shares[ring * REG_DEV + part] * source[part]
        mix[...] = (acc / total).T

    states = x_ref[:, :, column_block(o_ref)].reshape(MEMBER_TOTAL, o_ref.shape[-1])
    center = jnp.sum(states, axis=0, keepdims=True) * (1.0 / MEMBER_TOTAL)
    updated = center + dot(mix[...], states - center)
    o_ref[...] = updated.reshape(o_ref.shape)


def apply(cycle, region, place, nbr, factors, blend, prev, own, after, states):
    width = 512
    matrix = pl.BlockSpec(
        (REG_DEV, MEMBER_TOTAL, MEMBER_TOTAL), lambda i: (0, 0, 0), pipeline_mode=pl.Buffered(1)
    )
    tile = pl.BlockSpec((SHARES, SHARE, width), lambda i: (0, 0, i))
    return pl.pallas_call(
        functools.partial(apply_kernel, cycle, region),
        grid=(TILE_POINTS // width,),
        in_specs=[SMEM, SMEM, SMEM, SMEM, matrix, matrix, matrix, pl.BlockSpec(memory_space=pltpu.VMEM)],
        out_specs=tile,
        out_shape=pltpu.HBM((SHARES, SHARE, TILE_POINTS), jnp.float32),
        scratch_shapes=[pltpu.VMEM((MEMBER_TOTAL, MEMBER_TOTAL), jnp.float32)],
        compiler_params=pltpu.CompilerParams(vmem_limit_bytes=24 << 20),
        cost_estimate=pl.CostEstimate(
            flops=6 * 2 * 256 * 256 * TILE_POINTS, bytes_accessed=5 << 20, transcendentals=0
        ),
        name="apply",
    )(
        place,
        nbr,
        factors,
        blend,
        prev,
        own,
        after,
        pltpu.with_memory_space_constraint(states, pltpu.VMEM),
    )


def swap_pairs(bit):
    return [(i, i ^ bit) for i in range(SHARES)]


def gather_members(cells):
    index = lax.axis_index("member")
    block = cells[None]
    for bit in (1, 2, 4, 8):
        other = lax.ppermute(block, "member", swap_pairs(bit))
        upper = (index & bit) != 0
        block = jnp.concatenate(
            [jnp.where(upper, other, block), jnp.where(upper, block, other)], axis=0
        )
    return block


def from_beside(cells):
    count = lax.axis_size("region")
    before = lax.ppermute(cells, "region", [(i, (i + 1) % count) for i in range(count)])
    after = lax.ppermute(cells, "region", [((i + 1) % count, i) for i in range(count)])
    return before, after


def body(
    prior_states,
    prior_in_sensor_space,
    sensor_readings,
    error_precisions,
    live_tallies,
    adjacent_areas,
    taper_lookup,
    blend_lookup,
    taper_factors,
):
    cycle = lax.axis_size("region")
    place = lax.axis_index("region").astype(jnp.int32)[None]
    packed = [pack(prior_states, region) for region in range(REG_DEV)]
    own = gather_members(prior_in_sensor_space)
    packed[1], own = lax.optimization_barrier((packed[1], own))
    states = [lax.all_to_all(pieces, "member", 0, 0, tiled=True) for pieces in packed]
    before, after = from_beside(own)
    transforms = analysis(
        cycle,
        place,
        live_tallies,
        adjacent_areas,
        taper_factors,
        before,
        own,
        after,
        sensor_readings,
        error_precisions,
        taper_lookup,
    )
    left, right = from_beside(transforms)
    out = None
    for region in range(REG_DEV):
        updated = apply(
            cycle,
            region,
            place,
            adjacent_areas,
            taper_factors,
            blend_lookup,
            left,
            transforms,
            right,
            states[region],
        )
        back = lax.all_to_all(updated, "member", 0, 0, tiled=True)
        out = unpack(back, region, out)
    return out


def solution(mesh):
    placed = (
        P("region", "member", None, None),
        P("region", "member", None),
        P(),
        P(),
        P(),
        P(),
        P(),
        P("region", "member", None),
        P(),
    )
    return jax.shard_map(
        body,
        mesh=mesh,
        in_specs=placed,
        out_specs=P("region", "member", None, None),
        check_vma=False,
    )
```

time: 287 us -> 283 us (0.986); the launches traced: 282 us -> 281 us
  waiting for transfers between devices: 89.9 us -> 179 us
  blocking collectives: 55.8 us -> 0 us
  Pallas kernels: 0 us -> 47.9 us
  other arithmetic: 36 us -> 0.16 us
  matrix products: 31.7 us -> 0 us
  local copies, waits for them, and re-layouts: 28.5 us -> 3.91 us
  starting transfers between devices: 39.1 us -> 49.9 us
    all_to_all x1 -> x0, blocking collectives: 55.8 us -> none  [body(): back = lax.all_to_all(pieces, 'member', 0, 0, tiled=True)]
    ppermute x4 -> x8, waiting for transfers between devices: 39.7 us -> 91.4 us  [the longest x4 53.9 us: gather_members(): other = lax.ppermute(block, 'member', swap_pairs(bit))]
    pallas_call x0 -> x7, Pallas kernels: none -> 47.9 us  [the longest x1 24 us: analysis(): pl.pallas_call(functools.partial(analysis_kernel, cycle), grid_spec=pltpu...]
    all_to_all x4, waiting for transfers between devices: 50.1 us -> 88 us  [the longest x2 88 us: body(): back = lax.all_to_all(updated, 'member', 0, 0, tiled=True)]
    dot_general x29 -> x0, matrix products: 31.7 us -> none  [the longest x8 7.21 us: newton_root(): jnp.einsum('...ij,...jk->...ik', correction, root_mat, precision=highest)]
    ppermute x4 -> x8, starting transfers between devices: 2.86 us -> 14.9 us  [the longest x4 11.1 us: gather_members(): other = lax.ppermute(block, 'member', swap_pairs(bit))]
    gather x9 -> x0, local copies, waits for them, and re-layouts: 11.3 us -> none  [the longest x2 6.2 us: body(): picked = jnp.take(nearby, slot_table[region], axis=0)]
    mul x4 -> x0, other arithmetic: 10.8 us -> none  [the longest x1 9.95 us: body(): weight_sel = jnp.take(weight_cand, slot_table, axis=0) * loc_weight]
  transfers between devices with their start and end apart: 8 -> 12, of which waited for: 6 -> 10; matrix products, arithmetic and copies ran while one was open for 31% -> 0% of each run, Pallas kernels for 0% -> 14%
where the time goes in v2:
time: 283 us; the launch traced here: 281 us
  waiting for transfers between devices  179 us (63%)
  starting transfers between devices  49.9 us (18%)
  Pallas kernels  47.9 us (17%)
  local copies, waits for them, and re-layouts  3.91 us (1%)
    all_to_all x2, waiting for transfers between devices, body(): back = lax.all_to_all(updated, 'member', 0, 0, tiled=True)  88 us
    ppermute x4, waiting for transfers between devices, gather_members(): other = lax.ppermute(block, 'member', swap_pairs(bit))  53.9 us
    ppermute x2, waiting for transfers between devices, from_beside(): lax.ppermute(cells, 'region', [((i + 1) % count, i) for i in range(count)])  31 us
    pallas_call x1, Pallas kernels, analysis(): pl.pallas_call(functools.partial(analysis_kernel, cycle), grid_spec=pltpu...  24 us
    all_to_all x2, starting transfers between devices, body(): lax.all_to_all(pieces, 'member', 0, 0, tiled=True)  18.7 us
    all_to_all x2, starting transfers between devices, body(): back = lax.all_to_all(updated, 'member', 0, 0, tiled=True)  16.3 us
    ppermute x4, starting transfers between devices, gather_members(): other = lax.ppermute(block, 'member', swap_pairs(bit))  11.1 us
    pallas_call x2, Pallas kernels, apply(): pl.pallas_call(functools.partial(apply_kernel, cycle, region), grid=(TILE...  10.6 us
  transfers between devices with their start and end apart: 12, of which 10 were waited for; matrix products, arithmetic and copies ran while one was open for 0% of the time, Pallas kernels for 14%

profile of v2, /device:TPU:46, one launch (start us, length us, event | category | flops | bytes accessed | tf_op | source)
XLA Modules:
  0.0 281.5 jit_solution(11381722170651227118)
XLA Ops:
  0.0 3.9 %pack.3 = f32[16,16,2048]{2,1,0:T(8,128)} custom-call(f32[2,16,16,2048]{3,2,1,0:T(8,128)} %x_ref.3), custom_call_target="tpu_custom_call" | custom-call | bytes 4194304 | tf_op jit(solution)/shard_map/pack/pallas_call | solution.py:49
  3.9 9.6 %all-to-all-start.2 = ((f32[16,16,2048]{2,1,0:T(8,128)}), f32[16,16,2048]{2,1,0:T(8,128)S(1)}, u32[]{:S(2)}, u32[]{:S(2)}) async-start(f32[16,16,2048]{2,1,0:T(8,128)} %pack.3), calls=%async_computation.2 | async-start | bytes 4194304 | tf_op jit(solution)/shard_map/all_to_all | solution.py:288
  14.2 44.9 %collective-permute-done = f32[1,2,16,256]{3,2,1,0:T(8,128)S(1)} collective-permute-done((f32[1,2,16,256]{3,2,1,0:T(8,128)S(1)}, f32[1,2,16,256]{3,2,1,0:T(8,128)S(1)}, u32[]{:S(2)}, u32[]{:S(2)}) %collective-permute-start) | collective-permute-done | bytes 32800 | tf_op jit(solution)/shard_map/ppermute | solution.py:257
  59.1 4.1 %collective-permute-start.1 = (f32[2,2,16,256]{3,2,1,0:T(8,128)S(1)}, f32[2,2,16,256]{3,2,1,0:T(8,128)S(1)}, u32[]{:S(2)}, u32[]{:S(2)}) collective-permute-start(f32[2,2,16,256]{3,2,1,0:T(8,128)S(1)} %pad_maximum_fusion.3), channel_id=1, source_target_pairs={{0,2},{1,3},{2,0},{3,1},{4,6},{5,7},{6,4},{7,5},{8,10},{9,11},{10,... | collective-permute-start | bytes 196616 | tf_op jit(solution)/shard_map/ppermute | solution.py:257
  63.2 2.4 collective-permute-done.1
  65.6 5.4 %collective-permute-start.2 = (f32[4,2,16,256]{3,2,1,0:T(8,128)S(1)}, f32[4,2,16,256]{3,2,1,0:T(8,128)S(1)}, u32[]{:S(2)}, u32[]{:S(2)}) collective-permute-start(f32[4,2,16,256]{3,2,1,0:T(8,128)S(1)} %pad_maximum_fusion.2), channel_id=1, source_target_pairs={{0,4},{1,5},{2,6},{3,7},{4,0},{5,1},{6,2},{7,3},{8,12},{9,13},{10,... | collective-permute-start | bytes 393224 | tf_op jit(solution)/shard_map/ppermute | solution.py:257
  71.0 5.2 %collective-permute-done.2 = f32[4,2,16,256]{3,2,1,0:T(8,128)S(1)} collective-permute-done((f32[4,2,16,256]{3,2,1,0:T(8,128)S(1)}, f32[4,2,16,256]{3,2,1,0:T(8,128)S(1)}, u32[]{:S(2)}, u32[]{:S(2)}) %collective-permute-start.2) | collective-permute-done | bytes 131104 | tf_op jit(solution)/shard_map/ppermute | solution.py:257
  77.2 3.9 %pack.2 = f32[16,16,2048]{2,1,0:T(8,128)} custom-call(f32[2,16,16,2048]{3,2,1,0:T(8,128)} %x_ref.3), custom_call_target="tpu_custom_call" | custom-call | bytes 4194304 | tf_op jit(solution)/shard_map/pack/pallas_call | solution.py:49
  81.1 1.6 collective-permute-done.3
  82.8 9.1 %all-to-all-start = ((f32[16,16,2048]{2,1,0:T(8,128)}), f32[16,16,2048]{2,1,0:T(8,128)}, u32[]{:S(2)}, u32[]{:S(2)}) async-start(f32[16,16,2048]{2,1,0:T(8,128)} %pack.2), calls=%async_computation | async-start | bytes 4194304 | tf_op jit(solution)/shard_map/all_to_all | solution.py:288
  92.6 21.6 %collective-permute-done.5.next_ref = f32[16,2,16,256]{3,2,1,0:T(8,128)S(1)} collective-permute-done((f32[16,2,16,256]{3,2,1,0:T(8,128)S(1)}, f32[16,2,16,256]{3,2,1,0:T(8,128)S(1)}, u32[]{:S(2)}, u32[]{:S(2)}) %collective-permute-start.5) | collective-permute-done | bytes 524320 | tf_op jit(solution)/shard_map/ppermute | solution.py:268
  116.7 24.0 %analysis.1.own_ref = f32[2,256,256]{2,1,0:T(8,128)S(1)} custom-call(s32[1]{0:T(128)} %bitcast.place_ref, s32[32]{0:T(128)S(1)} %copy-done.7, s32[32,4]{1,0:T(8,128)S(1)} %copy.13.nbr_ref, f32[16]{0:T(128)S(1)} %copy-done.8, f32[16,2,16,256]{3,2,1,0:T(8,128)} %collective-permute-done.4.prev_ref, f32[16,2,16,256]{3,2,1,0:T(8,128)S(1)} %pad_maximum_fusion.own_ref, ...), custom_call_target="tpu_custom_call" | custom-call | flops 14092861440 | bytes 3145728 | tf_op jit(solution)/shard_map/analysis/pallas_call | solution.py:163
  140.7 3.3 %collective-permute-start.7 = (f32[2,256,256]{2,1,0:T(8,128)S(1)}, f32[2,256,256]{2,1,0:T(8,128)S(1)}, u32[]{:S(2)}, u32[]{:S(2)}) collective-permute-start(f32[2,256,256]{2,1,0:T(8,128)S(1)} %analysis.1.own_ref), channel_id=1, source_target_pairs={{16,0},{32,16},{48,32},{64,48},{80,64},{96,80},{112,96},{128,112},... | collective-permute-start | bytes 1572872 | tf_op jit(solution)/shard_map/ppermute | solution.py:268
  144.0 9.4 %collective-permute-done.7.next_ref = f32[2,256,256]{2,1,0:T(8,128)S(1)} collective-permute-done((f32[2,256,256]{2,1,0:T(8,128)S(1)}, f32[2,256,256]{2,1,0:T(8,128)S(1)}, u32[]{:S(2)}, u32[]{:S(2)}) %collective-permute-start.7) | collective-permute-done | bytes 524320 | tf_op jit(solution)/shard_map/ppermute | solution.py:268
  153.3 5.8 %collective-permute-done.6.prev_ref = f32[2,256,256]{2,1,0:T(8,128)S(1)} collective-permute-done((f32[2,256,256]{2,1,0:T(8,128)S(1)}, f32[2,256,256]{2,1,0:T(8,128)S(1)}, u32[]{:S(2)}, u32[]{:S(2)}) %collective-permute-start.6) | collective-permute-done | bytes 524320 | tf_op jit(solution)/shard_map/ppermute | solution.py:267
  159.2 4.9 %apply.3 = f32[16,16,2048]{2,1,0:T(8,128)} custom-call(s32[1]{0:T(128)} %bitcast.place_ref, s32[32,4]{1,0:T(8,128)S(1)} %copy.13.nbr_ref, f32[16]{0:T(128)S(1)} %copy-done.8, s32[2,1,5]{2,1,0:T(1,128)S(1)} %copy-done.6, f32[2,256,256]{2,1,0:T(8,128)S(1)} %collective-permute-done.6.prev_ref, f32[2,256,256]{2,1,0:T(8,128)S(1)} %analysis.1.own_ref, ...), custom_call_target="tpu_custom_call" | custom-call | flops 1610612736 | bytes 5242880 | tf_op jit(solution)/shard_map/apply/pallas_call | solution.py:225
  164.9 9.5 %all-to-all-start.3 = ((f32[16,16,2048]{2,1,0:T(8,128)}), f32[16,16,2048]{2,1,0:T(8,128)S(1)}, u32[]{:S(2)}, u32[]{:S(2)}) async-start(f32[16,16,2048]{2,1,0:T(8,128)} %apply.3), calls=%async_computation.3 | async-start | bytes 4194304 | tf_op jit(solution)/shard_map/all_to_all | solution.py:318
  174.4 1.0 copy-done.1
  175.5 5.7 %apply.2 = f32[16,16,2048]{2,1,0:T(8,128)} custom-call(s32[1]{0:T(128)} %bitcast.place_ref, s32[32,4]{1,0:T(8,128)S(1)} %copy.13.nbr_ref, f32[16]{0:T(128)S(1)} %copy-done.8, s32[2,1,5]{2,1,0:T(1,128)S(1)} %copy-done.6, f32[2,256,256]{2,1,0:T(8,128)S(1)} %copy-done.1, f32[2,256,256]{2,1,0:T(8,128)S(1)} %analysis.1.own_ref, ...), custom_call_target="tpu_custom_call" | custom-call | flops 1610612736 | bytes 5242880 | tf_op jit(solution)/shard_map/apply/pallas_call | solution.py:225
  181.1 41.7 %all-to-all-done.3.x_ref = f32[16,16,2048]{2,1,0:T(8,128)S(1)} async-done(((f32[16,16,2048]{2,1,0:T(8,128)}), f32[16,16,2048]{2,1,0:T(8,128)S(1)}, u32[]{:S(2)}, u32[]{:S(2)}) %all-to-all-start.3) | async-done | bytes 2097184 | tf_op jit(solution)/shard_map/all_to_all | solution.py:318
  222.8 6.8 %all-to-all-start.1 = ((f32[16,16,2048]{2,1,0:T(8,128)}), f32[16,16,2048]{2,1,0:T(8,128)}, u32[]{:S(2)}, u32[]{:S(2)}) async-start(f32[16,16,2048]{2,1,0:T(8,128)} %apply.2), calls=%async_computation.1 | async-start | bytes 4194304 | tf_op jit(solution)/shard_map/all_to_all | solution.py:318
  229.6 2.0 unpack.2.refs_0_
  231.6 46.3 %all-to-all-done.1.x_ref = f32[16,16,2048]{2,1,0:T(8,128)} async-done(((f32[16,16,2048]{2,1,0:T(8,128)}), f32[16,16,2048]{2,1,0:T(8,128)}, u32[]{:S(2)}, u32[]{:S(2)}) %all-to-all-start.1) | async-done | bytes 2097184 | tf_op jit(solution)/shard_map/all_to_all | solution.py:318
  277.9 3.6 %unpack.3 = f32[2,16,16,2048]{3,2,1,0:T(8,128)} custom-call(f32[16,16,2048]{2,1,0:T(8,128)} %all-to-all-done.1.x_ref, f32[2,16,16,2048]{3,2,1,0:T(8,128)} %unpack.2.refs_0_), custom_call_target="tpu_custom_call", output_to_operand_aliasing={{}: (1, {})} | custom-call | bytes 4194304 | tf_op jit(solution)/shard_map/unpack/pallas_call | solution.py:67
  (41 shorter events, 5.8 us)
Async XLA Ops:
  3.9 9.6 %copy-start.10 = (f32[2,16,256]{2,1,0:T(8,128)S(1)}, f32[2,16,256]{2,1,0:T(8,128)}, u32[]{:S(2)}) copy-start(f32[2,16,256]{2,1,0:T(8,128)} %param.10) | copy-start | bytes 98308
  3.9 78.9 %all-to-all-start.2 = ((f32[16,16,2048]{2,1,0:T(8,128)}), f32[16,16,2048]{2,1,0:T(8,128)S(1)}, u32[]{:S(2)}, u32[]{:S(2)}) async-start(f32[16,16,2048]{2,1,0:T(8,128)} %pack.3), calls=%async_computation.2 | async-start | bytes 4194304 | tf_op jit(solution)/shard_map/all_to_all | solution.py:288
  13.6 45.5 %collective-permute-start = (f32[1,2,16,256]{3,2,1,0:T(8,128)S(1)}, f32[1,2,16,256]{3,2,1,0:T(8,128)S(1)}, u32[]{:S(2)}, u32[]{:S(2)}) collective-permute-start(f32[1,2,16,256]{3,2,1,0:T(8,128)S(1)} %bitcast.4), channel_id=1, source_target_pairs={{0,1},{1,0},{2,3},{3,2},{4,5},{5,4},{6,7},{7,6},{8,9},{9,8},{10,11... | collective-permute-start | bytes 98312 | tf_op jit(solution)/shard_map/ppermute | solution.py:257
  59.1 6.5 %collective-permute-start.1 = (f32[2,2,16,256]{3,2,1,0:T(8,128)S(1)}, f32[2,2,16,256]{3,2,1,0:T(8,128)S(1)}, u32[]{:S(2)}, u32[]{:S(2)}) collective-permute-start(f32[2,2,16,256]{3,2,1,0:T(8,128)S(1)} %pad_maximum_fusion.3), channel_id=1, source_target_pairs={{0,2},{1,3},{2,0},{3,1},{4,6},{5,7},{6,4},{7,5},{8,10},{9,11},{10,... | collective-permute-start | bytes 196616 | tf_op jit(solution)/shard_map/ppermute | solution.py:257
  65.6 10.5 %collective-permute-start.2 = (f32[4,2,16,256]{3,2,1,0:T(8,128)S(1)}, f32[4,2,16,256]{3,2,1,0:T(8,128)S(1)}, u32[]{:S(2)}, u32[]{:S(2)}) collective-permute-start(f32[4,2,16,256]{3,2,1,0:T(8,128)S(1)} %pad_maximum_fusion.2), channel_id=1, source_target_pairs={{0,4},{1,5},{2,6},{3,7},{4,0},{5,1},{6,2},{7,3},{8,12},{9,13},{10,... | collective-permute-start | bytes 393224 | tf_op jit(solution)/shard_map/ppermute | solution.py:257
  76.2 6.5 %collective-permute-start.3 = (f32[8,2,16,256]{3,2,1,0:T(8,128)S(1)}, f32[8,2,16,256]{3,2,1,0:T(8,128)S(1)}, u32[]{:S(2)}, u32[]{:S(2)}) collective-permute-start(f32[8,2,16,256]{3,2,1,0:T(8,128)S(1)} %pad_maximum_fusion.1), channel_id=1, source_target_pairs={{0,8},{1,9},{2,10},{3,11},{4,12},{5,13},{6,14},{7,15},{8,0},{9,1},... | collective-permute-start | bytes 786440 | tf_op jit(solution)/shard_map/ppermute | solution.py:257
  82.7 9.7 %copy-start.11 = (s32[32,4]{0,1:T(4,128)S(1)}, s32[32,4]{0,1:T(4,128)}, u32[]{:S(2)}) copy-start(s32[32,4]{0,1:T(4,128)} %param.14) | copy-start | bytes 1540
  82.7 9.8 %copy-start.9 = (s32[32,5,256]{2,0,1:T(8,128)S(1)}, s32[32,5,256]{2,0,1:T(8,128)}, u32[]{:S(2)}) copy-start(s32[32,5,256]{2,0,1:T(8,128)} %param.15) | copy-start | bytes 491524
  82.7 32.9 %copy-start.4 = (f32[32,256]{1,0:T(8,128)S(1)}, f32[32,256]{1,0:T(8,128)}, u32[]{:S(2)}) copy-start(f32[32,256]{1,0:T(8,128)} %values_ref.1) | copy-start | bytes 98308
  82.8 32.9 %copy-start.5 = (f32[32,256]{1,0:T(8,128)S(1)}, f32[32,256]{1,0:T(8,128)}, u32[]{:S(2)}) copy-start(f32[32,256]{1,0:T(8,128)} %precision_ref.1) | copy-start | bytes 98308
  82.8 32.9 %copy-start.7 = (s32[32]{0:T(128)S(1)}, s32[32]{0:T(128)}, u32[]{:S(2)}) copy-start(s32[32]{0:T(128)} %live_ref.1) | copy-start | bytes 388
  82.8 32.9 %copy-start.8 = (f32[16]{0:T(128)S(1)}, f32[16]{0:T(128)}, u32[]{:S(2)}) copy-start(f32[16]{0:T(128)} %factor_ref.5) | copy-start | bytes 196
  82.8 82.1 %all-to-all-start = ((f32[16,16,2048]{2,1,0:T(8,128)}), f32[16,16,2048]{2,1,0:T(8,128)}, u32[]{:S(2)}, u32[]{:S(2)}) async-start(f32[16,16,2048]{2,1,0:T(8,128)} %pack.2), calls=%async_computation | async-start | bytes 4194304 | tf_op jit(solution)/shard_map/all_to_all | solution.py:288
  91.9 22.3 %collective-permute-start.5 = (f32[16,2,16,256]{3,2,1,0:T(8,128)S(1)}, f32[16,2,16,256]{3,2,1,0:T(8,128)S(1)}, u32[]{:S(2)}, u32[]{:S(2)}) collective-permute-start(f32[16,2,16,256]{3,2,1,0:T(8,128)S(1)} %pad_maximum_fusion.own_ref), channel_id=1, source_target_pairs={{16,0},{32,16},{48,32},{64,48},{80,64},{96,80},{112,96},{128,112},... | collective-permute-start | bytes 1572872 | tf_op jit(solution)/shard_map/ppermute | solution.py:268
  91.9 23.7 %collective-permute-start.4 = (f32[16,2,16,256]{3,2,1,0:T(8,128)S(1)}, f32[16,2,16,256]{3,2,1,0:T(8,128)}, u32[]{:S(2)}, u32[]{:S(2)}) collective-permute-start(f32[16,2,16,256]{3,2,1,0:T(8,128)S(1)} %pad_maximum_fusion.own_ref), channel_id=1, source_target_pairs={{0,16},{16,32},{32,48},{48,64},{64,80},{80,96},{96,112},{112,128},... | collective-permute-start | bytes 1572872 | tf_op jit(solution)/shard_map/ppermute | solution.py:267
  114.2 0.8 copy-start.2
  115.7 1.0 copy-start.3
  116.7 42.5 %copy-start.6 = (s32[2,1,5]{2,1,0:T(1,128)S(1)}, s32[2,1,5]{2,1,0:T(1,128)}, u32[]{:S(2)}) copy-start(s32[2,1,5]{2,1,0:T(1,128)} %blend_ref.3) | copy-start | bytes 124
  140.7 12.6 %collective-permute-start.7 = (f32[2,256,256]{2,1,0:T(8,128)S(1)}, f32[2,256,256]{2,1,0:T(8,128)S(1)}, u32[]{:S(2)}, u32[]{:S(2)}) collective-permute-start(f32[2,256,256]{2,1,0:T(8,128)S(1)} %analysis.1.own_ref), channel_id=1, source_target_pairs={{16,0},{32,16},{48,32},{64,48},{80,64},{96,80},{112,96},{128,112},... | collective-permute-start | bytes 1572872 | tf_op jit(solution)/shard_map/ppermute | solution.py:268
  144.0 15.2 %collective-permute-start.6 = (f32[2,256,256]{2,1,0:T(8,128)S(1)}, f32[2,256,256]{2,1,0:T(8,128)S(1)}, u32[]{:S(2)}, u32[]{:S(2)}) collective-permute-start(f32[2,256,256]{2,1,0:T(8,128)S(1)} %analysis.1.own_ref), channel_id=1, source_target_pairs={{0,16},{16,32},{32,48},{48,64},{64,80},{80,96},{96,112},{112,128},... | collective-permute-start | bytes 1572872 | tf_op jit(solution)/shard_map/ppermute | solution.py:267
  164.1 0.8 copy-start
  164.9 57.9 %all-to-all-start.3 = ((f32[16,16,2048]{2,1,0:T(8,128)}), f32[16,16,2048]{2,1,0:T(8,128)S(1)}, u32[]{:S(2)}, u32[]{:S(2)}) async-start(f32[16,16,2048]{2,1,0:T(8,128)} %apply.3), calls=%async_computation.3 | async-start | bytes 4194304 | tf_op jit(solution)/shard_map/all_to_all | solution.py:318
  174.4 1.0 copy-start.1
  222.8 55.1 %all-to-all-start.1 = ((f32[16,16,2048]{2,1,0:T(8,128)}), f32[16,16,2048]{2,1,0:T(8,128)}, u32[]{:S(2)}, u32[]{:S(2)}) async-start(f32[16,16,2048]{2,1,0:T(8,128)} %apply.2), calls=%async_computation.1 | async-start | bytes 4194304 | tf_op jit(solution)/shard_map/all_to_all | solution.py:318

commit v3 on v2

v3 whole, which is shorter than its diff:
```python
import functools

import jax
import jax.numpy as jnp
from jax import lax
from jax.experimental import pallas as pl
from jax.experimental.pallas import tpu as pltpu
from jax.sharding import PartitionSpec as P

MEMBER_TOTAL = 256
NOBS = 256
NBR = 4
NSIT = 8
REG_DEV = 2
LEVELS = 16
TILE_POINTS = 2048
SHARES = 16
SHARE = 16
RINGS = 8

inflation = 1.1
highest = lax.Precision.HIGHEST
SMEM = pl.BlockSpec(memory_space=pltpu.SMEM)


def dot(a, b):
    return lax.dot_general(
        a, b, (((1,), (0,)), ((), ())), precision=highest, preferred_element_type=jnp.float32
    )


def dot_rows(a, b):
    return lax.dot_general(
        a, b, (((1,), (1,)), ((), ())), precision=highest, preferred_element_type=jnp.float32
    )


WIDTH = 512
HALF = SHARE // 2

LISTED = [0, 7, 1, 6, 2, 5, 3, 4, 12, 11, 13, 10, 14, 9, 15, 8]
PLACE = [LISTED.index(member) for member in range(SHARES)]


def columns(number):
    return pl.ds(number * WIDTH, WIDTH)


def pack_kernel(x_ref, o_ref):
    for number in range(TILE_POINTS // WIDTH):
        by_patch = jnp.swapaxes(x_ref[0, :, :, columns(number)], 0, 1)
        for place, patch in enumerate(LISTED):
            o_ref[place, 0, :, columns(number)] = by_patch[patch]


def pack(states):
    return pl.pallas_call(
        pack_kernel,
        grid=(REG_DEV, SHARE // HALF),
        in_specs=[pl.BlockSpec((1, HALF, SHARES, TILE_POINTS), lambda r, i: (r, i, 0, 0))],
        out_specs=pl.BlockSpec((SHARES, 1, HALF, TILE_POINTS), lambda r, i: (0, r, i, 0)),
        out_shape=pltpu.HBM((SHARES, REG_DEV, SHARE, TILE_POINTS), jnp.float32),
        cost_estimate=pl.CostEstimate(flops=0, bytes_accessed=8 << 20, transcendentals=0),
        name="pack",
    )(states)


def unpack_kernel(x_ref, *refs):
    o_ref = refs[-1]
    for number in range(TILE_POINTS // WIDTH):
        pieces = x_ref[:, :, columns(number)]
        by_patch = jnp.stack([pieces[PLACE[patch]] for patch in range(SHARES)])
        o_ref[0, :, :, columns(number)] = jnp.swapaxes(by_patch, 0, 1)


def unpack(pieces, region, target=None):
    extra = [] if target is None else [target]
    return pl.pallas_call(
        unpack_kernel,
        grid=(SHARE // HALF,),
        in_specs=[pl.BlockSpec((SHARES, HALF, TILE_POINTS), lambda i: (0, i, 0))]
        + [pl.BlockSpec(memory_space=pl.ANY)] * len(extra),
        out_specs=pl.BlockSpec((1, HALF, SHARES, TILE_POINTS), lambda i: (region, i, 0, 0)),
        out_shape=jax.ShapeDtypeStruct((REG_DEV, SHARE, SHARES, TILE_POINTS), jnp.float32),
        input_output_aliases={1: 0} if extra else {},
        cost_estimate=pl.CostEstimate(flops=0, bytes_accessed=4 << 20, transcendentals=0),
        name="unpack",
    )(pltpu.with_memory_space_constraint(pieces, pltpu.HBM), *extra)


def slot_of(area, place, cycle):
    ring = lax.rem(area // REG_DEV - place + 1 + cycle, cycle)
    return ring * REG_DEV + lax.rem(area, REG_DEV)


def area_of(block, row, neighbours):
    return row if block == 0 else neighbours[row, block - 1]


def analysis_kernel(
    cycle,
    place_ref,
    live_ref,
    nbr_ref,
    factor_ref,
    prev_near,
    prev_far,
    own_near,
    own_far,
    next_near,
    next_far,
    values_ref,
    precision_ref,
    lookup_ref,
    out_ref,
    pert,
    mean,
    scaled,
    root,
):
    place = place_ref[0]
    half = MEMBER_TOTAL // 2
    for ring, source in enumerate(
        ((prev_near, prev_far), (own_near, own_far), (next_near, next_far))
    ):
        for part in range(REG_DEV):
            slot = ring * REG_DEV + part
            blocks = [ref[:, part].reshape(half, NOBS) for ref in source]
            total = sum(jnp.sum(block, axis=0, keepdims=True) for block in blocks)
            average = total * (1.0 / MEMBER_TOTAL)
            for side, block in enumerate(blocks):
                pert[slot, pl.ds(side * half, half), :] = block - average
            mean[slot] = jnp.broadcast_to(average, (8, NOBS))
    slots = lax.broadcasted_iota(jnp.int32, (1, NOBS), 1)
    rows = lax.broadcasted_iota(jnp.int32, (MEMBER_TOTAL, MEMBER_TOTAL), 0)
    cols = lax.broadcasted_iota(jnp.int32, (MEMBER_TOTAL, MEMBER_TOTAL), 1)
    identity = jnp.where(rows == cols, 1.0, 0.0).astype(jnp.float32)
    drives, norms = [], []
    for region in range(REG_DEV):
        row = place * REG_DEV + region
        lookup = lookup_ref[region]
        taper = jnp.zeros(lookup.shape, jnp.float32)
        for level in range(LEVELS):
            taper = jnp.where(lookup == level, factor_ref[level], taper)
        gram = ((MEMBER_TOTAL - 1) / inflation) * identity
        drive = jnp.zeros((MEMBER_TOTAL, 128), jnp.float32)
        for block in range(NBR + 1):
            area = area_of(block, row, nbr_ref)
            slot = slot_of(area, place, cycle)
            weight = jnp.where(slots < live_ref[area], precision_ref[pl.ds(area, 1), :], 0.0)
            weight = weight * taper[block : block + 1, :]
            offset = values_ref[pl.ds(area, 1), :] - mean[slot][0:1, :]
            block_pert = pert[slot]
            gram = gram + dot_rows(block_pert * weight, block_pert)
            drive = drive + dot_rows(
                block_pert, jnp.broadcast_to(weight * offset, (128, NOBS))
            )
        norm = jnp.sqrt(jnp.sum(gram * gram, keepdims=True))
        first = gram / norm
        step = 1.5 * identity - 0.5 * first
        root[region] = step
        scaled[region] = dot(first, step)
        drives.append(drive)
        norms.append(norm)

    def sweep(_, carry):
        steps = [
            1.5 * identity - 0.5 * dot(root[region], scaled[region]) for region in range(REG_DEV)
        ]
        roots = [dot(steps[region], root[region]) for region in range(REG_DEV)]
        scales = [dot(scaled[region], steps[region]) for region in range(REG_DEV)]
        for region in range(REG_DEV):
            root[region] = roots[region]
            scaled[region] = scales[region]
        return carry

    lax.fori_loop(0, NSIT - 2, sweep, 0)
    for region in range(REG_DEV):
        root_mat = root[region]
        step = 1.5 * identity - 0.5 * dot(root_mat, scaled[region])
        root_mat = dot(step, root_mat)
        shift = dot(root_mat, dot(root_mat, drives[region])) / norms[region]
        factor = jnp.sqrt(jnp.float32(MEMBER_TOTAL - 1)) / jnp.sqrt(norms[region])
        out_ref[region] = factor * root_mat + jnp.concatenate([shift, shift], axis=1)


def analysis(cycle, place, live, nbr, factors, cells, values, precisions, lookup):
    whole = lambda *shape: pl.BlockSpec(shape, lambda i, *_: (0,) * len(shape))
    areas = values.shape[0]
    return pl.pallas_call(
        functools.partial(analysis_kernel, cycle),
        grid_spec=pltpu.PrefetchScalarGridSpec(
            num_scalar_prefetch=4,
            grid=(1,),
            in_specs=[whole(RINGS, REG_DEV, SHARE, NOBS)] * len(cells)
            + [
                whole(areas, NOBS),
                whole(areas, NOBS),
                pl.BlockSpec((REG_DEV, NBR + 1, NOBS), lambda i, p, *_: (p[0], 0, 0)),
            ],
            out_specs=whole(REG_DEV, MEMBER_TOTAL, MEMBER_TOTAL),
            scratch_shapes=[
                pltpu.VMEM((3 * REG_DEV, MEMBER_TOTAL, NOBS), jnp.float32),
                pltpu.VMEM((3 * REG_DEV, 8, NOBS), jnp.float32),
                pltpu.VMEM((REG_DEV, MEMBER_TOTAL, MEMBER_TOTAL), jnp.float32),
                pltpu.VMEM((REG_DEV, MEMBER_TOTAL, MEMBER_TOTAL), jnp.float32),
            ],
        ),
        out_shape=jax.ShapeDtypeStruct((REG_DEV, MEMBER_TOTAL, MEMBER_TOTAL), jnp.float32),
        compiler_params=pltpu.CompilerParams(vmem_limit_bytes=24 << 20),
        cost_estimate=pl.CostEstimate(
            flops=60 * 6 * 2 * 256**3, bytes_accessed=3 << 20, transcendentals=0
        ),
        name="analysis",
    )(place, live, nbr, factors, *cells, values, precisions, lookup)


def apply_kernel(
    cycle,
    region,
    place_ref,
    nbr_ref,
    factor_ref,
    blend_ref,
    order_ref,
    prev_ref,
    own_ref,
    next_ref,
    x_ref,
    o_ref,
    mix,
    cells,
):
    @pl.when(pl.program_id(0) == 0)
    def _():
        place = place_ref[0]
        row = place * REG_DEV + region
        shares = [jnp.float32(0.0)] * (3 * REG_DEV)
        total = jnp.float32(0.0)
        for block in range(NBR + 1):
            slot = slot_of(area_of(block, row, nbr_ref), place, cycle)
            value = factor_ref[blend_ref[region, 0, block]]
            total = total + value
            shares = [s + jnp.where(slot == k, value, 0.0) for k, s in enumerate(shares)]
        acc = jnp.zeros((MEMBER_TOTAL, MEMBER_TOTAL), jnp.float32)
        for ring, source in enumerate((prev_ref, own_ref, next_ref)):
            for part in range(REG_DEV):
                acc = acc + shares[ring * REG_DEV + part] * source[part]
        mix[...] = (acc / total).T

    here = pl.ds(pl.multiple_of(pl.program_id(0) * WIDTH, WIDTH), WIDTH)
    for rank in range(SHARES):
        cells[pl.ds(rank * SHARE, SHARE), :] = x_ref[order_ref[rank], region, :, here]
    states = cells[...]
    center = jnp.sum(states, axis=0, keepdims=True) * (1.0 / MEMBER_TOTAL)
    updated = center + dot(mix[...], states - center)
    for rank in range(SHARES):
        o_ref[order_ref[rank]] = updated[rank * SHARE : (rank + 1) * SHARE, :]


def apply(cycle, region, scalars, beside, states):
    matrix = pl.BlockSpec(
        (REG_DEV, MEMBER_TOTAL, MEMBER_TOTAL), lambda i: (0, 0, 0), pipeline_mode=pl.Buffered(1)
    )
    return pl.pallas_call(
        functools.partial(apply_kernel, cycle, region),
        grid=(TILE_POINTS // WIDTH,),
        in_specs=[SMEM] * 5 + [matrix] * 3 + [pl.BlockSpec(memory_space=pltpu.VMEM)],
        out_specs=pl.BlockSpec((SHARES, SHARE, WIDTH), lambda i: (0, 0, i)),
        out_shape=pltpu.HBM((SHARES, SHARE, TILE_POINTS), jnp.float32),
        scratch_shapes=[
            pltpu.VMEM((MEMBER_TOTAL, MEMBER_TOTAL), jnp.float32),
            pltpu.VMEM((MEMBER_TOTAL, WIDTH), jnp.float32),
        ],
        compiler_params=pltpu.CompilerParams(vmem_limit_bytes=24 << 20),
        cost_estimate=pl.CostEstimate(
            flops=6 * 2 * 256 * 256 * TILE_POINTS, bytes_accessed=5 << 20, transcendentals=0
        ),
        name="apply",
    )(*scalars, *beside, pltpu.with_memory_space_constraint(states, pltpu.VMEM))


def member_at(index, along_x, along_z):
    columns = SHARES // RINGS
    return (index // RINGS + along_x) % columns * RINGS + (index + along_z) % RINGS


RING_ORDER = (0, 4, 1, 5, 2, 6, 7, 3)


def traded(pieces):
    return lax.all_to_all(pieces, "member", 0, 0, axis_index_groups=[LISTED], tiled=True)


def from_ring(cells):
    def sent(piece, step):
        return lax.ppermute(
            piece, "member", [(i, member_at(i, 0, step)) for i in range(SHARES)]
        )

    pair = jnp.stack([cells, sent(cells, 4)])
    return jnp.concatenate([pair] + [sent(pair, step) for step in (1, 2, 7)])


def from_around(near):
    count = lax.axis_size("region")
    got = []
    for shift in (1, 0, -1):
        for across in (0, 1):
            if shift == 0 and across == 0:
                got.append(near)
                continue
            pairs = [
                (g * SHARES + i, (g + shift) % count * SHARES + member_at(i, across, 0))
                for g in range(count)
                for i in range(SHARES)
            ]
            got.append(lax.ppermute(near, ("region", "member"), pairs))
    return got


def from_beside(cells):
    count = lax.axis_size("region")
    before = lax.ppermute(cells, "region", [(i, (i + 1) % count) for i in range(count)])
    after = lax.ppermute(cells, "region", [((i + 1) % count, i) for i in range(count)])
    return before, after


def body(
    prior_states,
    prior_in_sensor_space,
    sensor_readings,
    error_precisions,
    live_tallies,
    adjacent_areas,
    taper_lookup,
    blend_lookup,
    taper_factors,
):
    cycle = lax.axis_size("region")
    place = lax.axis_index("region").astype(jnp.int32)[None]
    index = lax.axis_index("member").astype(jnp.int32)
    order = jnp.stack(
        [member_at(index, across, -step) for across in (0, 1) for step in RING_ORDER]
    )
    order = jnp.take(jnp.array(PLACE, jnp.int32), order)
    near = from_ring(prior_in_sensor_space)
    packed = pack(prior_states)
    packed, near = lax.optimization_barrier((packed, near))
    cells = from_around(near)
    states = traded(packed)
    transforms = analysis(
        cycle,
        place,
        live_tallies,
        adjacent_areas,
        taper_factors,
        cells,
        sensor_readings,
        error_precisions,
        taper_lookup,
    )
    left, right = from_beside(transforms)
    scalars = (place, adjacent_areas, taper_factors, blend_lookup, order)
    beside = (left, transforms, right)
    out = None
    for region in range(REG_DEV):
        updated = apply(cycle, region, scalars, beside, states)
        out = unpack(traded(updated), region, out)
    return out


def solution(mesh):
    placed = (
        P("region", "member", None, None),
        P("region", "member", None),
        P(),
        P(),
        P(),
        P(),
        P(),
        P("region", "member", None),
        P(),
    )
    return jax.shard_map(
        body,
        mesh=mesh,
        in_specs=placed,
        out_specs=P("region", "member", None, None),
        check_vma=False,
    )
```

time: 283 us -> 239 us (0.84)
  waiting for transfers between devices: 179 us -> 147 us
  starting transfers between devices: 49.9 us -> 42.9 us
  Pallas kernels: 47.9 us -> 42.9 us
    ppermute x2 -> x1, waiting for transfers between devices: 31 us -> 10.9 us  [from_beside(): lax.ppermute(cells, 'region', [((i + 1) % count, i) for i in range(count)])]
    ppermute x4 -> x9, waiting for transfers between devices: 53.9 us -> 40.1 us  [the longest x5 36.9 us: from_around(): got.append(lax.ppermute(near, ('region', 'member'), pairs))]
    all_to_all x4 -> x3, starting transfers between devices: 35 us -> 25.4 us  [traded(): lax.all_to_all(pieces, 'member', 0, 0, axis_index_groups=[LISTED], tiled=...]
    ppermute x4 -> x9, starting transfers between devices: 11.1 us -> 16.5 us  [the longest x4 11.1 us: sent(): lax.ppermute(piece, 'member', [(i, member_at(i, 0, step)) for i in range(...]
    ppermute x2 -> x1, waiting for transfers between devices: 6.48 us -> 11.7 us  [from_beside(): lax.ppermute(cells, 'region', [(i, (i + 1) % count) for i in range(count)])]
    pallas_call x1, Pallas kernels: 24 us -> 20 us  [analysis(): pl.pallas_call(functools.partial(analysis_kernel, cycle), grid_spec=pltpu...]
    all_to_all x4 -> x3, waiting for transfers between devices: 88 us -> 84.2 us  [traded(): lax.all_to_all(pieces, 'member', 0, 0, axis_index_groups=[LISTED], tiled=...]
    pallas_call x4 -> x3, Pallas kernels: 13.4 us -> 10.4 us  [the longest x2 5.48 us: unpack(): pl.pallas_call(unpack_kernel, grid=(SHARE // HALF,), in_specs=[pl.BlockSp...]
  transfers between devices with their start and end apart: 12 -> 14, of which waited for: 10 -> 10; matrix products, arithmetic and copies ran while one was open for 0% -> 1% of each run, Pallas kernels for 14% -> 14%
where the time goes in v3:
time: 239 us; the launch traced here: 235 us
  waiting for transfers between devices  147 us (62%)
  starting transfers between devices  42.9 us (18%)
  Pallas kernels  42.9 us (18%)
    all_to_all x3, waiting for transfers between devices, traded(): lax.all_to_all(pieces, 'member', 0, 0, axis_index_groups=[LISTED], tiled=...  84.2 us
    ppermute x5, waiting for transfers between devices, from_around(): got.append(lax.ppermute(near, ('region', 'member'), pairs))  36.9 us
    all_to_all x3, starting transfers between devices, traded(): lax.all_to_all(pieces, 'member', 0, 0, axis_index_groups=[LISTED], tiled=...  25.4 us
    pallas_call x1, Pallas kernels, analysis(): pl.pallas_call(functools.partial(analysis_kernel, cycle), grid_spec=pltpu...  20 us
    pallas_call x2, Pallas kernels, apply(): pl.pallas_call(functools.partial(apply_kernel, cycle, region), grid=(TILE...  12.6 us
    ppermute x1, waiting for transfers between devices, from_beside(): lax.ppermute(cells, 'region', [(i, (i + 1) % count) for i in range(count)])  11.7 us
    ppermute x4, starting transfers between devices, sent(): lax.ppermute(piece, 'member', [(i, member_at(i, 0, step)) for i in range(...  11.1 us
    ppermute x1, waiting for transfers between devices, from_beside(): lax.ppermute(cells, 'region', [((i + 1) % count, i) for i in range(count)])  10.9 us
  transfers between devices with their start and end apart: 14, of which 10 were waited for; matrix products, arithmetic and copies ran while one was open for 1% of the time, Pallas kernels for 14%

profile of v3, /device:TPU:46, one launch (start us, length us, event | category | flops | bytes accessed | tf_op | source)
XLA Modules:
  0.0 234.7 jit_solution(14079159228105563533)
XLA Ops:
  0.0 6.3 %collective-permute-start = (f32[2,16,256]{2,1,0:T(8,128)}, f32[2,16,256]{2,1,0:T(8,128)S(1)}, u32[]{:S(2)}, u32[]{:S(2)}) collective-permute-start(f32[2,16,256]{2,1,0:T(8,128)} %param.11), channel_id=1, source_target_pairs={{0,4},{1,5},{2,6},{3,7},{4,0},{5,1},{6,2},{7,3},{8,12},{9,13},{10,... | collective-permute-start | bytes 98312 | tf_op jit(solution)/shard_map/ppermute | solution.py:297
  7.1 4.9 %pack.1 = f32[16,2,16,2048]{3,2,1,0:T(8,128)} custom-call(f32[2,16,16,2048]{3,2,1,0:T(8,128)} %x_ref.1), custom_call_target="tpu_custom_call" | custom-call | bytes 8388608 | tf_op jit(solution)/shard_map/pack/pallas_call | solution.py:57
  13.1 1.5 collective-permute-start.2
  14.6 2.2 collective-permute-start.1
  16.8 3.1 %collective-permute-done.1 = f32[2,2,16,256]{3,2,1,0:T(8,128)S(1)} collective-permute-done((f32[2,2,16,256]{3,2,1,0:T(8,128)S(1)}, f32[2,2,16,256]{3,2,1,0:T(8,128)S(1)}, u32[]{:S(2)}, u32[]{:S(2)}) %collective-permute-start.1) | collective-permute-done | bytes 65568 | tf_op jit(solution)/shard_map/ppermute | solution.py:297
  20.1 7.0 %all-to-all-start = ((f32[16,2,16,2048]{3,2,1,0:T(8,128)}), f32[16,2,16,2048]{3,2,1,0:T(8,128)}, u32[]{:S(2)}, u32[]{:S(2)}) async-start(f32[16,2,16,2048]{3,2,1,0:T(8,128)} %pack.1), calls=%async_computation | async-start | bytes 8388608 | tf_op jit(solution)/shard_map/all_to_all | solution.py:292
  27.1 1.7 collective-permute-start.7
  29.7 2.9 %collective-permute-start.4 = (f32[8,2,16,256]{3,2,1,0:T(8,128)S(1)}, f32[8,2,16,256]{3,2,1,0:T(8,128)S(1)}, u32[]{:S(2)}, u32[]{:S(2)}) collective-permute-start(f32[8,2,16,256]{3,2,1,0:T(8,128)S(1)} %constant_dynamic-update-slice_fusion.own_near), channel_id=1, source_target_pairs={{0,16},{1,17},{2,18},{3,19},{4,20},{5,21},{6,22},{7,23},{8,24},{9,... | collective-permute-start | bytes 786440 | tf_op jit(solution)/shard_map/ppermute | solution.py:318
  32.9 2.8 %collective-permute-done.8.next_far = f32[8,2,16,256]{3,2,1,0:T(8,128)S(1)} collective-permute-done((f32[8,2,16,256]{3,2,1,0:T(8,128)S(1)}, f32[8,2,16,256]{3,2,1,0:T(8,128)S(1)}, u32[]{:S(2)}, u32[]{:S(2)}) %collective-permute-start.8) | collective-permute-done | bytes 262176 | tf_op jit(solution)/shard_map/ppermute | solution.py:318
  35.7 25.5 %collective-permute-done.7.next_near = f32[8,2,16,256]{3,2,1,0:T(8,128)S(1)} collective-permute-done((f32[8,2,16,256]{3,2,1,0:T(8,128)S(1)}, f32[8,2,16,256]{3,2,1,0:T(8,128)S(1)}, u32[]{:S(2)}, u32[]{:S(2)}) %collective-permute-start.7) | collective-permute-done | bytes 262176 | tf_op jit(solution)/shard_map/ppermute | solution.py:318
  61.2 5.6 %collective-permute-done.6.own_far = f32[8,2,16,256]{3,2,1,0:T(8,128)S(1)} collective-permute-done((f32[8,2,16,256]{3,2,1,0:T(8,128)S(1)}, f32[8,2,16,256]{3,2,1,0:T(8,128)S(1)}, u32[]{:S(2)}, u32[]{:S(2)}) %collective-permute-start.6) | collective-permute-done | bytes 262176 | tf_op jit(solution)/shard_map/ppermute | solution.py:318
  66.8 3.0 %collective-permute-done.5.prev_far = f32[8,2,16,256]{3,2,1,0:T(8,128)S(1)} collective-permute-done((f32[8,2,16,256]{3,2,1,0:T(8,128)S(1)}, f32[8,2,16,256]{3,2,1,0:T(8,128)S(1)}, u32[]{:S(2)}, u32[]{:S(2)}) %collective-permute-start.5) | collective-permute-done | bytes 262176 | tf_op jit(solution)/shard_map/ppermute | solution.py:318
  69.9 20.0 %analysis.1.own_ref = f32[2,256,256]{2,1,0:T(8,128)S(1)} custom-call(s32[1]{0:T(128)} %bitcast.place_ref, s32[32]{0:T(128)S(1)} %copy-done.4, s32[32,4]{1,0:T(8,128)S(1)} %copy.18.nbr_ref, f32[16]{0:T(128)S(1)} %copy-done.1, f32[8,2,16,256]{3,2,1,0:T(8,128)S(1)} %collective-permute-done.4.prev_near, f32[8,2,16,256]{3,2,1,0:T(8,128)S(1)} %collective-permute-done.5.prev_far, ...), custom_call_target="tpu_custom_call" | custom-call | flops 12079595520 | bytes 3145728 | tf_op jit(solution)/shard_map/analysis/pallas_call | solution.py:190
  91.6 10.9 %collective-permute-done.10.next_ref = f32[2,256,256]{2,1,0:T(8,128)S(1)} collective-permute-done((f32[2,256,256]{2,1,0:T(8,128)S(1)}, f32[2,256,256]{2,1,0:T(8,128)S(1)}, u32[]{:S(2)}, u32[]{:S(2)}) %collective-permute-start.10) | collective-permute-done | bytes 524320 | tf_op jit(solution)/shard_map/ppermute | solution.py:325
  102.5 11.7 %collective-permute-done.9.prev_ref = f32[2,256,256]{2,1,0:T(8,128)S(1)} collective-permute-done((f32[2,256,256]{2,1,0:T(8,128)S(1)}, f32[2,256,256]{2,1,0:T(8,128)S(1)}, u32[]{:S(2)}, u32[]{:S(2)}) %collective-permute-start.9) | collective-permute-done | bytes 524320 | tf_op jit(solution)/shard_map/ppermute | solution.py:324
  114.1 2.7 %all-to-all-done.x_ref = f32[16,2,16,2048]{3,2,1,0:T(8,128)} async-done(((f32[16,2,16,2048]{3,2,1,0:T(8,128)}), f32[16,2,16,2048]{3,2,1,0:T(8,128)}, u32[]{:S(2)}, u32[]{:S(2)}) %all-to-all-start) | async-done | bytes 4194336 | tf_op jit(solution)/shard_map/all_to_all | solution.py:292
  116.8 6.2 %apply.3 = f32[16,16,2048]{2,1,0:T(8,128)} custom-call(s32[1]{0:T(128)} %bitcast.place_ref, s32[32,4]{1,0:T(8,128)S(1)} %copy.18.nbr_ref, f32[16]{0:T(128)S(1)} %copy-done.1, s32[2,1,5]{2,1,0:T(1,128)S(1)} %copy-done, s32[16]{0:T(128)S(1)} %and_select_fusion.order_ref, f32[2,256,256]{2,1,0:T(8,128)S(1)} %collective-permute-done.9.prev_ref, ...), custom_call_target="tpu_custom_call" | custom-call | flops 1610612736 | bytes 5242880 | tf_op jit(solution)/shard_map/apply/pallas_call | solution.py:265
  123.0 9.7 %all-to-all-start.2 = ((f32[16,16,2048]{2,1,0:T(8,128)}), f32[16,16,2048]{2,1,0:T(8,128)}, u32[]{:S(2)}, u32[]{:S(2)}) async-start(f32[16,16,2048]{2,1,0:T(8,128)} %apply.3), calls=%async_computation.2 | async-start | bytes 4194304 | tf_op jit(solution)/shard_map/all_to_all | solution.py:292
  132.6 6.4 %apply.2 = f32[16,16,2048]{2,1,0:T(8,128)} custom-call(s32[1]{0:T(128)} %bitcast.place_ref, s32[32,4]{1,0:T(8,128)S(1)} %copy.18.nbr_ref, f32[16]{0:T(128)S(1)} %copy-done.1, s32[2,1,5]{2,1,0:T(1,128)S(1)} %copy-done, s32[16]{0:T(128)S(1)} %and_select_fusion.order_ref, f32[2,256,256]{2,1,0:T(8,128)S(1)} %collective-permute-done.9.prev_ref, ...), custom_call_target="tpu_custom_call" | custom-call | flops 1610612736 | bytes 5242880 | tf_op jit(solution)/shard_map/apply/pallas_call | solution.py:265
  139.0 38.7 %all-to-all-done.2.x_ref = f32[16,16,2048]{2,1,0:T(8,128)} async-done(((f32[16,16,2048]{2,1,0:T(8,128)}), f32[16,16,2048]{2,1,0:T(8,128)}, u32[]{:S(2)}, u32[]{:S(2)}) %all-to-all-start.2) | async-done | bytes 2097184 | tf_op jit(solution)/shard_map/all_to_all | solution.py:292
  177.7 8.7 %all-to-all-start.1 = ((f32[16,16,2048]{2,1,0:T(8,128)}), f32[16,16,2048]{2,1,0:T(8,128)}, u32[]{:S(2)}, u32[]{:S(2)}) async-start(f32[16,16,2048]{2,1,0:T(8,128)} %apply.2), calls=%async_computation.1 | async-start | bytes 4194304 | tf_op jit(solution)/shard_map/all_to_all | solution.py:292
  186.4 2.7 %unpack.2.refs_0_ = f32[2,16,16,2048]{3,2,1,0:T(8,128)} custom-call(f32[16,16,2048]{2,1,0:T(8,128)} %all-to-all-done.2.x_ref), custom_call_target="tpu_custom_call" | custom-call | bytes 4194304 | tf_op jit(solution)/shard_map/unpack/pallas_call | solution.py:78
  189.1 42.8 %all-to-all-done.1.x_ref = f32[16,16,2048]{2,1,0:T(8,128)} async-done(((f32[16,16,2048]{2,1,0:T(8,128)}), f32[16,16,2048]{2,1,0:T(8,128)}, u32[]{:S(2)}, u32[]{:S(2)}) %all-to-all-start.1) | async-done | bytes 2097184 | tf_op jit(solution)/shard_map/all_to_all | solution.py:292
  231.9 2.7 %unpack.3 = f32[2,16,16,2048]{3,2,1,0:T(8,128)} custom-call(f32[16,16,2048]{2,1,0:T(8,128)} %all-to-all-done.1.x_ref, f32[2,16,16,2048]{3,2,1,0:T(8,128)} %unpack.2.refs_0_), custom_call_target="tpu_custom_call", output_to_operand_aliasing={{}: (1, {})} | custom-call | bytes 4194304 | tf_op jit(solution)/shard_map/unpack/pallas_call | solution.py:78
  (42 shorter events, 4.9 us)
Async XLA Ops:
  0.0 12.0 %collective-permute-start = (f32[2,16,256]{2,1,0:T(8,128)}, f32[2,16,256]{2,1,0:T(8,128)S(1)}, u32[]{:S(2)}, u32[]{:S(2)}) collective-permute-start(f32[2,16,256]{2,1,0:T(8,128)} %param.11), channel_id=1, source_target_pairs={{0,4},{1,5},{2,6},{3,7},{4,0},{5,1},{6,2},{7,3},{8,12},{9,13},{10,... | collective-permute-start | bytes 98312 | tf_op jit(solution)/shard_map/ppermute | solution.py:297
  7.1 4.9 %copy-start.7 = (f32[2,16,256]{2,1,0:T(8,128)S(1)}, f32[2,16,256]{2,1,0:T(8,128)}, u32[]{:S(2)}) copy-start(f32[2,16,256]{2,1,0:T(8,128)} %param.11) | copy-start | bytes 98308
  12.0 7.9 %collective-permute-start.3 = (f32[2,2,16,256]{3,2,1,0:T(8,128)S(1)}, f32[2,2,16,256]{3,2,1,0:T(8,128)S(1)}, u32[]{:S(2)}, u32[]{:S(2)}) collective-permute-start(f32[2,2,16,256]{3,2,1,0:T(8,128)S(1)} %pad_maximum_fusion), channel_id=1, source_target_pairs={{0,7},{1,0},{2,1},{3,2},{4,3},{5,4},{6,5},{7,6},{8,15},{9,8},{10,9... | collective-permute-start | bytes 196616 | tf_op jit(solution)/shard_map/ppermute | solution.py:297
  13.1 6.8 %collective-permute-start.2 = (f32[2,2,16,256]{3,2,1,0:T(8,128)S(1)}, f32[2,2,16,256]{3,2,1,0:T(8,128)S(1)}, u32[]{:S(2)}, u32[]{:S(2)}) collective-permute-start(f32[2,2,16,256]{3,2,1,0:T(8,128)S(1)} %pad_maximum_fusion), channel_id=1, source_target_pairs={{0,2},{1,3},{2,4},{3,5},{4,6},{5,7},{6,0},{7,1},{8,10},{9,11},{10,... | collective-permute-start | bytes 196616 | tf_op jit(solution)/shard_map/ppermute | solution.py:297
  14.6 5.4 %collective-permute-start.1 = (f32[2,2,16,256]{3,2,1,0:T(8,128)S(1)}, f32[2,2,16,256]{3,2,1,0:T(8,128)S(1)}, u32[]{:S(2)}, u32[]{:S(2)}) collective-permute-start(f32[2,2,16,256]{3,2,1,0:T(8,128)S(1)} %pad_maximum_fusion), channel_id=1, source_target_pairs={{0,1},{1,2},{2,3},{3,4},{4,5},{5,6},{6,7},{7,0},{8,9},{9,10},{10,1... | collective-permute-start | bytes 196616 | tf_op jit(solution)/shard_map/ppermute | solution.py:297
  20.0 12.5 %copy-start.8 = (s32[32,4]{0,1:T(4,128)S(1)}, s32[32,4]{0,1:T(4,128)}, u32[]{:S(2)}) copy-start(s32[32,4]{0,1:T(4,128)} %param.15) | copy-start | bytes 1540
  20.0 12.6 %copy-start.6 = (s32[32,5,256]{2,0,1:T(8,128)S(1)}, s32[32,5,256]{2,0,1:T(8,128)}, u32[]{:S(2)}) copy-start(s32[32,5,256]{2,0,1:T(8,128)} %param.16) | copy-start | bytes 491524
  20.0 49.8 %copy-start.1 = (f32[16]{0:T(128)S(1)}, f32[16]{0:T(128)}, u32[]{:S(2)}) copy-start(f32[16]{0:T(128)} %factor_ref.5) | copy-start | bytes 196
  20.0 49.8 %copy-start.2 = (f32[32,256]{1,0:T(8,128)S(1)}, f32[32,256]{1,0:T(8,128)}, u32[]{:S(2)}) copy-start(f32[32,256]{1,0:T(8,128)} %values_ref.1) | copy-start | bytes 98308
  20.1 49.8 %copy-start.3 = (f32[32,256]{1,0:T(8,128)S(1)}, f32[32,256]{1,0:T(8,128)}, u32[]{:S(2)}) copy-start(f32[32,256]{1,0:T(8,128)} %precision_ref.1) | copy-start | bytes 98308
  20.1 49.8 %copy-start.4 = (s32[32]{0:T(128)S(1)}, s32[32]{0:T(128)}, u32[]{:S(2)}) copy-start(s32[32]{0:T(128)} %live_ref.1) | copy-start | bytes 388
  20.1 96.7 %all-to-all-start = ((f32[16,2,16,2048]{3,2,1,0:T(8,128)}), f32[16,2,16,2048]{3,2,1,0:T(8,128)}, u32[]{:S(2)}, u32[]{:S(2)}) async-start(f32[16,2,16,2048]{3,2,1,0:T(8,128)} %pack.1), calls=%async_computation | async-start | bytes 8388608 | tf_op jit(solution)/shard_map/all_to_all | solution.py:292
  27.1 8.6 %collective-permute-start.8 = (f32[8,2,16,256]{3,2,1,0:T(8,128)S(1)}, f32[8,2,16,256]{3,2,1,0:T(8,128)S(1)}, u32[]{:S(2)}, u32[]{:S(2)}) collective-permute-start(f32[8,2,16,256]{3,2,1,0:T(8,128)S(1)} %constant_dynamic-update-slice_fusion.own_near), channel_id=1, source_target_pairs={{0,248},{1,249},{2,250},{3,251},{4,252},{5,253},{6,254},{7,255},{8... | collective-permute-start | bytes 786440 | tf_op jit(solution)/shard_map/ppermute | solution.py:318
  27.1 34.0 %collective-permute-start.7 = (f32[8,2,16,256]{3,2,1,0:T(8,128)S(1)}, f32[8,2,16,256]{3,2,1,0:T(8,128)S(1)}, u32[]{:S(2)}, u32[]{:S(2)}) collective-permute-start(f32[8,2,16,256]{3,2,1,0:T(8,128)S(1)} %constant_dynamic-update-slice_fusion.own_near), channel_id=1, source_target_pairs={{0,240},{1,241},{2,242},{3,243},{4,244},{5,245},{6,246},{7,247},{8... | collective-permute-start | bytes 786440 | tf_op jit(solution)/shard_map/ppermute | solution.py:318
  28.8 38.0 %collective-permute-start.6 = (f32[8,2,16,256]{3,2,1,0:T(8,128)S(1)}, f32[8,2,16,256]{3,2,1,0:T(8,128)S(1)}, u32[]{:S(2)}, u32[]{:S(2)}) collective-permute-start(f32[8,2,16,256]{3,2,1,0:T(8,128)S(1)} %constant_dynamic-update-slice_fusion.own_near), channel_id=1, source_target_pairs={{0,8},{1,9},{2,10},{3,11},{4,12},{5,13},{6,14},{7,15},{8,0},{9,1},... | collective-permute-start | bytes 786440 | tf_op jit(solution)/shard_map/ppermute | solution.py:318
  29.7 40.2 %collective-permute-start.5 = (f32[8,2,16,256]{3,2,1,0:T(8,128)S(1)}, f32[8,2,16,256]{3,2,1,0:T(8,128)S(1)}, u32[]{:S(2)}, u32[]{:S(2)}) collective-permute-start(f32[8,2,16,256]{3,2,1,0:T(8,128)S(1)} %constant_dynamic-update-slice_fusion.own_near), channel_id=1, source_target_pairs={{0,24},{1,25},{2,26},{3,27},{4,28},{5,29},{6,30},{7,31},{8,16},{9,... | collective-permute-start | bytes 786440 | tf_op jit(solution)/shard_map/ppermute | solution.py:318
  29.7 40.2 %collective-permute-start.4 = (f32[8,2,16,256]{3,2,1,0:T(8,128)S(1)}, f32[8,2,16,256]{3,2,1,0:T(8,128)S(1)}, u32[]{:S(2)}, u32[]{:S(2)}) collective-permute-start(f32[8,2,16,256]{3,2,1,0:T(8,128)S(1)} %constant_dynamic-update-slice_fusion.own_near), channel_id=1, source_target_pairs={{0,16},{1,17},{2,18},{3,19},{4,20},{5,21},{6,22},{7,23},{8,24},{9,... | collective-permute-start | bytes 786440 | tf_op jit(solution)/shard_map/ppermute | solution.py:318
  69.8 21.0 %copy-start.5 = (s32[16]{0:T(128)S(1)}, s32[16]{0:T(128)}, u32[]{:S(2)}) copy-start(s32[16]{0:T(128)} %constant.179.clone) | copy-start | bytes 196
  69.8 46.9 %copy-start = (s32[2,1,5]{2,1,0:T(1,128)S(1)}, s32[2,1,5]{2,1,0:T(1,128)}, u32[]{:S(2)}) copy-start(s32[2,1,5]{2,1,0:T(1,128)} %blend_ref.3) | copy-start | bytes 124
  89.8 12.6 %collective-permute-start.10 = (f32[2,256,256]{2,1,0:T(8,128)S(1)}, f32[2,256,256]{2,1,0:T(8,128)S(1)}, u32[]{:S(2)}, u32[]{:S(2)}) collective-permute-start(f32[2,256,256]{2,1,0:T(8,128)S(1)} %analysis.1.own_ref), channel_id=1, source_target_pairs={{16,0},{32,16},{48,32},{64,48},{80,64},{96,80},{112,96},{128,112},... | collective-permute-start | bytes 1572872 | tf_op jit(solution)/shard_map/ppermute | solution.py:325
  90.8 23.3 %collective-permute-start.9 = (f32[2,256,256]{2,1,0:T(8,128)S(1)}, f32[2,256,256]{2,1,0:T(8,128)S(1)}, u32[]{:S(2)}, u32[]{:S(2)}) collective-permute-start(f32[2,256,256]{2,1,0:T(8,128)S(1)} %analysis.1.own_ref), channel_id=1, source_target_pairs={{0,16},{16,32},{32,48},{48,64},{64,80},{80,96},{96,112},{112,128},... | collective-permute-start | bytes 1572872 | tf_op jit(solution)/shard_map/ppermute | solution.py:324
  123.0 54.7 %all-to-all-start.2 = ((f32[16,16,2048]{2,1,0:T(8,128)}), f32[16,16,2048]{2,1,0:T(8,128)}, u32[]{:S(2)}, u32[]{:S(2)}) async-start(f32[16,16,2048]{2,1,0:T(8,128)} %apply.3), calls=%async_computation.2 | async-start | bytes 4194304 | tf_op jit(solution)/shard_map/all_to_all | solution.py:292
  177.7 54.3 %all-to-all-start.1 = ((f32[16,16,2048]{2,1,0:T(8,128)}), f32[16,16,2048]{2,1,0:T(8,128)}, u32[]{:S(2)}, u32[]{:S(2)}) async-start(f32[16,16,2048]{2,1,0:T(8,128)} %apply.2), calls=%async_computation.1 | async-start | bytes 4194304 | tf_op jit(solution)/shard_map/all_to_all | solution.py:292

commit v4 on v3

--- a/solution.py
+++ b/solution.py
@@ -36,56 +36,68 @@
 
 
 WIDTH = 512
+SIDES = SHARES // RINGS
+
+LISTED = [0, 2, 5, 1, 7, 4, 3, 6]
+ALL_LISTED = [0, 7, 1, 6, 2, 5, 3, 4, 12, 11, 13, 10, 14, 9, 15, 8]
 HALF = SHARE // 2
-
-LISTED = [0, 7, 1, 6, 2, 5, 3, 4, 12, 11, 13, 10, 14, 9, 15, 8]
-PLACE = [LISTED.index(member) for member in range(SHARES)]
 
 
 def columns(number):
     return pl.ds(number * WIDTH, WIDTH)
 
 
-def pack_kernel(x_ref, o_ref):
+def pack_kernel(x_ref, *refs):
+    o_ref = refs[-1]
     for number in range(TILE_POINTS // WIDTH):
         by_patch = jnp.swapaxes(x_ref[0, :, :, columns(number)], 0, 1)
-        for place, patch in enumerate(LISTED):
+        for place, patch in enumerate(ALL_LISTED):
             o_ref[place, 0, :, columns(number)] = by_patch[patch]
 
 
-def pack(states):
+def pack(states, region, target=None):
+    extra = [] if target is None else [target]
     return pl.pallas_call(
         pack_kernel,
-        grid=(REG_DEV, SHARE // HALF),
-        in_specs=[pl.BlockSpec((1, HALF, SHARES, TILE_POINTS), lambda r, i: (r, i, 0, 0))],
-        out_specs=pl.BlockSpec((SHARES, 1, HALF, TILE_POINTS), lambda r, i: (0, r, i, 0)),
+        grid=(SHARE // HALF,),
+        in_specs=[pl.BlockSpec((1, HALF, SHARES, TILE_POINTS), lambda i: (region, i, 0, 0))]
+        + [pl.BlockSpec(memory_space=pl.ANY)] * len(extra),
+        out_specs=pl.BlockSpec((SHARES, 1, HALF, TILE_POINTS), lambda i: (0, region, i, 0)),
         out_shape=pltpu.HBM((SHARES, REG_DEV, SHARE, TILE_POINTS), jnp.float32),
-        cost_estimate=pl.CostEstimate(flops=0, bytes_accessed=8 << 20, transcendentals=0),
+        input_output_aliases={1: 0} if extra else {},
+        cost_estimate=pl.CostEstimate(flops=0, bytes_accessed=4 << 20, transcendentals=0),
         name="pack",
-    )(states)
-
-
-def unpack_kernel(x_ref, *refs):
+    )(states, *extra)
+
+
+def unpack_kernel(_, x_ref, *refs):
     o_ref = refs[-1]
     for number in range(TILE_POINTS // WIDTH):
-        pieces = x_ref[:, :, columns(number)]
-        by_patch = jnp.stack([pieces[PLACE[patch]] for patch in range(SHARES)])
+        pieces = x_ref[:, 0, :, columns(number)]
+        by_patch = jnp.stack([pieces[LISTED.index(patch)] for patch in range(RINGS)])
         o_ref[0, :, :, columns(number)] = jnp.swapaxes(by_patch, 0, 1)
 
 
-def unpack(pieces, region, target=None):
+def unpack(region, sides, pieces, target=None):
     extra = [] if target is None else [target]
     return pl.pallas_call(
         unpack_kernel,
-        grid=(SHARE // HALF,),
-        in_specs=[pl.BlockSpec((SHARES, HALF, TILE_POINTS), lambda i: (0, i, 0))]
-        + [pl.BlockSpec(memory_space=pl.ANY)] * len(extra),
-        out_specs=pl.BlockSpec((1, HALF, SHARES, TILE_POINTS), lambda i: (region, i, 0, 0)),
+        grid_spec=pltpu.PrefetchScalarGridSpec(
+            num_scalar_prefetch=1,
+            grid=sides.shape,
+            in_specs=[
+                pl.BlockSpec((RINGS, 1, SHARE, TILE_POINTS), lambda k, sides: (0, k, 0, 0))
+            ]
+            + [pl.BlockSpec(memory_space=pl.ANY)] * len(extra),
+            out_specs=pl.BlockSpec(
+                (1, SHARE, RINGS, TILE_POINTS), lambda k, sides: (region, 0, sides[k], 0)
+            ),
+        ),
         out_shape=jax.ShapeDtypeStruct((REG_DEV, SHARE, SHARES, TILE_POINTS), jnp.float32),
-        input_output_aliases={1: 0} if extra else {},
+        input_output_aliases={2: 0} if extra else {},
         cost_estimate=pl.CostEstimate(flops=0, bytes_accessed=4 << 20, transcendentals=0),
         name="unpack",
-    )(pltpu.with_memory_space_constraint(pieces, pltpu.HBM), *extra)
+    )(sides, pltpu.with_memory_space_constraint(pieces, pltpu.HBM), *extra)
 
 
 def slot_of(area, place, cycle):
@@ -95,6 +107,9 @@
 
 def area_of(block, row, neighbours):
     return row if block == 0 else neighbours[row, block - 1]
+
+
+EXTRA = 8
 
 
 def analysis_kernel(
@@ -175,13 +190,19 @@
         return carry
 
     lax.fori_loop(0, NSIT - 2, sweep, 0)
+    roots, extra = [], []
     for region in range(REG_DEV):
         root_mat = root[region]
         step = 1.5 * identity - 0.5 * dot(root_mat, scaled[region])
         root_mat = dot(step, root_mat)
         shift = dot(root_mat, dot(root_mat, drives[region])) / norms[region]
         factor = jnp.sqrt(jnp.float32(MEMBER_TOTAL - 1)) / jnp.sqrt(norms[region])
-        out_ref[region] = factor * root_mat + jnp.concatenate([shift, shift], axis=1)
+        roots.append(factor * root_mat)
+        extra.append(shift.T[0:1, :])
+    out_ref[pl.ds(0, MEMBER_TOTAL), :] = jnp.where(rows <= cols, roots[0], roots[1])
+    diagonal = jnp.sum(roots[1] * identity, axis=0, keepdims=True)
+    blank = jnp.zeros((EXTRA - 3, MEMBER_TOTAL), jnp.float32)
+    out_ref[pl.ds(MEMBER_TOTAL, EXTRA), :] = jnp.concatenate([*extra, diagonal, blank])
 
 
 def analysis(cycle, place, live, nbr, factors, cells, values, precisions, lookup):
@@ -198,7 +219,7 @@
                 whole(areas, NOBS),
                 pl.BlockSpec((REG_DEV, NBR + 1, NOBS), lambda i, p, *_: (p[0], 0, 0)),
             ],
-            out_specs=whole(REG_DEV, MEMBER_TOTAL, MEMBER_TOTAL),
+            out_specs=whole(MEMBER_TOTAL + EXTRA, MEMBER_TOTAL),
             scratch_shapes=[
                 pltpu.VMEM((3 * REG_DEV, MEMBER_TOTAL, NOBS), jnp.float32),
                 pltpu.VMEM((3 * REG_DEV, 8, NOBS), jnp.float32),
@@ -206,7 +227,7 @@
                 pltpu.VMEM((REG_DEV, MEMBER_TOTAL, MEMBER_TOTAL), jnp.float32),
             ],
         ),
-        out_shape=jax.ShapeDtypeStruct((REG_DEV, MEMBER_TOTAL, MEMBER_TOTAL), jnp.float32),
+        out_shape=jax.ShapeDtypeStruct((MEMBER_TOTAL + EXTRA, MEMBER_TOTAL), jnp.float32),
         compiler_params=pltpu.CompilerParams(vmem_limit_bytes=24 << 20),
         cost_estimate=pl.CostEstimate(
             flops=60 * 6 * 2 * 256**3, bytes_accessed=3 << 20, transcendentals=0
@@ -215,25 +236,23 @@
     )(place, live, nbr, factors, *cells, values, precisions, lookup)
 
 
-def apply_kernel(
+def blend_kernel(
     cycle,
-    region,
     place_ref,
     nbr_ref,
     factor_ref,
     blend_ref,
-    order_ref,
+    enter_ref,
+    leave_ref,
     prev_ref,
     own_ref,
     next_ref,
-    x_ref,
     o_ref,
-    mix,
-    cells,
 ):
-    @pl.when(pl.program_id(0) == 0)
-    def _():
-        place = place_ref[0]
+    place = place_ref[0]
+    rows = lax.broadcasted_iota(jnp.int32, (MEMBER_TOTAL, MEMBER_TOTAL), 0)
+    cols = lax.broadcasted_iota(jnp.int32, (MEMBER_TOTAL, MEMBER_TOTAL), 1)
+    for region in range(REG_DEV):
         row = place * REG_DEV + region
         shares = [jnp.float32(0.0)] * (3 * REG_DEV)
         total = jnp.float32(0.0)
@@ -242,42 +261,73 @@
             value = factor_ref[blend_ref[region, 0, block]]
             total = total + value
             shares = [s + jnp.where(slot == k, value, 0.0) for k, s in enumerate(shares)]
-        acc = jnp.zeros((MEMBER_TOTAL, MEMBER_TOTAL), jnp.float32)
+        square = pl.ds(0, MEMBER_TOTAL)
+        upper = jnp.zeros((MEMBER_TOTAL, MEMBER_TOTAL), jnp.float32)
+        lower = upper
+        shift = jnp.zeros((1, MEMBER_TOTAL), jnp.float32)
+        diagonal = shift
         for ring, source in enumerate((prev_ref, own_ref, next_ref)):
-            for part in range(REG_DEV):
-                acc = acc + shares[ring * REG_DEV + part] * source[part]
-        mix[...] = (acc / total).T
-
-    here = pl.ds(pl.multiple_of(pl.program_id(0) * WIDTH, WIDTH), WIDTH)
-    for rank in range(SHARES):
-        cells[pl.ds(rank * SHARE, SHARE), :] = x_ref[order_ref[rank], region, :, here]
-    states = cells[...]
+            first, second = shares[ring * REG_DEV : (ring + 1) * REG_DEV]
+            upper = upper + first * source[square, :]
+            lower = lower + second * source[square, :]
+            below = source[pl.ds(MEMBER_TOTAL, EXTRA), :]
+            shift = shift + first * below[0:1, :] + second * below[1:2, :]
+            diagonal = diagonal + second * below[2:3, :]
+        joined = jnp.where(rows <= cols, upper, lower)
+        mirrored = jnp.where(rows == cols, diagonal, joined.T)
+        mixed = ((joined + mirrored + shift) / total).T
+        for order_ref in (enter_ref, leave_ref):
+            for rank in range(SHARES):
+                first = pl.multiple_of(order_ref[rank] * SHARE, SHARE)
+                o_ref[region, pl.ds(first, SHARE), :] = mixed[rank * SHARE : (rank + 1) * SHARE, :]
+            if order_ref is enter_ref:
+                mixed = o_ref[region].T
+
+
+def blend(cycle, scalars, beside):
+    return pl.pallas_call(
+        functools.partial(blend_kernel, cycle),
+        in_specs=[SMEM] * 6 + [pl.BlockSpec(memory_space=pltpu.VMEM)] * 3,
+        out_specs=pl.BlockSpec(memory_space=pltpu.VMEM),
+        out_shape=jax.ShapeDtypeStruct((REG_DEV, MEMBER_TOTAL, MEMBER_TOTAL), jnp.float32),
+        compiler_params=pltpu.CompilerParams(vmem_limit_bytes=24 << 20),
+        cost_estimate=pl.CostEstimate(
+            flops=24 * 256 * 256, bytes_accessed=2 << 20, transcendentals=0
+        ),
+        name="blend",
+    )(*scalars, *beside)
+
+
+def apply_kernel(mix_ref, x_ref, *o_refs):
+    half = MEMBER_TOTAL // SIDES
+    states = x_ref[:, 0].reshape(MEMBER_TOTAL, WIDTH)
     center = jnp.sum(states, axis=0, keepdims=True) * (1.0 / MEMBER_TOTAL)
-    updated = center + dot(mix[...], states - center)
-    for rank in range(SHARES):
-        o_ref[order_ref[rank]] = updated[rank * SHARE : (rank + 1) * SHARE, :]
-
-
-def apply(cycle, region, scalars, beside, states):
-    matrix = pl.BlockSpec(
-        (REG_DEV, MEMBER_TOTAL, MEMBER_TOTAL), lambda i: (0, 0, 0), pipeline_mode=pl.Buffered(1)
-    )
+    updated = center + dot(mix_ref[0], states - center)
+    for side in range(SIDES):
+        part = updated[side * half : (side + 1) * half].reshape(RINGS, SHARE, WIDTH)
+        if len(o_refs) == 1:
+            o_refs[0][:, side] = part
+        else:
+            o_refs[side][:, 0] = part
+
+
+def apply(mixed, region, states, arrays):
+    sides = SIDES // arrays
     return pl.pallas_call(
-        functools.partial(apply_kernel, cycle, region),
+        apply_kernel,
         grid=(TILE_POINTS // WIDTH,),
-        in_specs=[SMEM] * 5 + [matrix] * 3 + [pl.BlockSpec(memory_space=pltpu.VMEM)],
-        out_specs=pl.BlockSpec((SHARES, SHARE, WIDTH), lambda i: (0, 0, i)),
-        out_shape=pltpu.HBM((SHARES, SHARE, TILE_POINTS), jnp.float32),
-        scratch_shapes=[
-            pltpu.VMEM((MEMBER_TOTAL, MEMBER_TOTAL), jnp.float32),
-            pltpu.VMEM((MEMBER_TOTAL, WIDTH), jnp.float32),
+        in_specs=[
+            pl.BlockSpec((1, MEMBER_TOTAL, MEMBER_TOTAL), lambda i: (region, 0, 0)),
+            pl.BlockSpec((SHARES, 1, SHARE, WIDTH), lambda i: (0, region, 0, i)),
         ],
+        out_specs=[pl.BlockSpec((RINGS, sides, SHARE, WIDTH), lambda i: (0, 0, 0, i))] * arrays,
+        out_shape=[pltpu.HBM((RINGS, sides, SHARE, TILE_POINTS), jnp.float32)] * arrays,
         compiler_params=pltpu.CompilerParams(vmem_limit_bytes=24 << 20),
         cost_estimate=pl.CostEstimate(
             flops=6 * 2 * 256 * 256 * TILE_POINTS, bytes_accessed=5 << 20, transcendentals=0
         ),
         name="apply",
-    )(*scalars, *beside, pltpu.with_memory_space_constraint(states, pltpu.VMEM))
+    )(mixed, pltpu.with_memory_space_constraint(states, pltpu.HBM))
 
 
 def member_at(index, along_x, along_z):
@@ -288,18 +338,38 @@
 RING_ORDER = (0, 4, 1, 5, 2, 6, 7, 3)
 
 
+def listed_at(members, listed):
+    place = jnp.zeros(members.shape, jnp.int32)
+    for number, member in enumerate(listed):
+        place = jnp.where(members == member, number, place)
+    return place
+
+
+def traded_by_all(pieces):
+    return lax.all_to_all(pieces, "member", 0, 0, axis_index_groups=[ALL_LISTED], tiled=True)
+
+
 def traded(pieces):
-    return lax.all_to_all(pieces, "member", 0, 0, axis_index_groups=[LISTED], tiled=True)
-
-
-def from_ring(cells):
+    groups = [[side * RINGS + along for along in LISTED] for side in range(SIDES)]
+    return lax.all_to_all(pieces, "member", 0, 0, axis_index_groups=groups, tiled=True)
+
+
+def across(pieces):
+    return lax.ppermute(pieces, "member", [(i, member_at(i, 1, 0)) for i in range(SHARES)])
+
+
+def from_ring(cells, states):
     def sent(piece, step):
         return lax.ppermute(
             piece, "member", [(i, member_at(i, 0, step)) for i in range(SHARES)]
         )
 
     pair = jnp.stack([cells, sent(cells, 4)])
-    return jnp.concatenate([pair] + [sent(pair, step) for step in (1, 2, 7)])
+    packed, pair = lax.optimization_barrier((pack(states, 0), pair))
+    packed = pack(states, 1, packed)
+    pieces = [sent(pair, step) for step in (1, 2, 7)]
+    packed, pieces = lax.optimization_barrier((packed, pieces))
+    return jnp.concatenate([pair] + pieces), packed
 
 
 def from_around(near):
@@ -340,15 +410,16 @@
     cycle = lax.axis_size("region")
     place = lax.axis_index("region").astype(jnp.int32)[None]
     index = lax.axis_index("member").astype(jnp.int32)
-    order = jnp.stack(
-        [member_at(index, across, -step) for across in (0, 1) for step in RING_ORDER]
-    )
-    order = jnp.take(jnp.array(PLACE, jnp.int32), order)
-    near = from_ring(prior_in_sensor_space)
-    packed = pack(prior_states)
-    packed, near = lax.optimization_barrier((packed, near))
+    along = (index % RINGS - jnp.array(RING_ORDER, jnp.int32)) % RINGS
+    here = index // RINGS
+    leave = listed_at(along, LISTED)
+    leave = jnp.concatenate([leave, RINGS + leave])
+    enter = jnp.concatenate([here * RINGS + along, (1 - here) * RINGS + along])
+    enter = listed_at(enter, ALL_LISTED)
+    here, there = here[None], 1 - here[None]
+    near, packed = from_ring(prior_in_sensor_space, prior_states)
     cells = from_around(near)
-    states = traded(packed)
+    states = traded_by_all(packed)
     transforms = analysis(
         cycle,
         place,
@@ -361,13 +432,17 @@
         taper_lookup,
     )
     left, right = from_beside(transforms)
-    scalars = (place, adjacent_areas, taper_factors, blend_lookup, order)
-    beside = (left, transforms, right)
-    out = None
-    for region in range(REG_DEV):
-        updated = apply(cycle, region, scalars, beside, states)
-        out = unpack(traded(updated), region, out)
-    return out
+    scalars = (place, adjacent_areas, taper_factors, blend_lookup, enter, leave)
+    mixed = blend(cycle, scalars, (left, transforms, right))
+    (leaving,) = apply(mixed, 0, states, 1)
+    first = traded(leaving)
+    near, far = apply(mixed, 1, states, 2)
+    both = jnp.concatenate([near, across(far)], axis=1)
+    both, first = lax.optimization_barrier((both, first))
+    second = traded(both)
+    out = unpack(0, here, first)
+    out = unpack(0, there, across(first[:, 1:]), out)
+    return unpack(1, jnp.concatenate([here, there]), second, out)
 
 
 def solution(mesh):

time: 239 us -> 237 us (level); the launches traced: 235 us -> 236 us
  other arithmetic: 0.02 us -> 3.66 us
  starting transfers between devices: 42.9 us -> 39.8 us
  Pallas kernels: 42.9 us -> 45.6 us
    ppermute x0 -> x2, waiting for transfers between devices: none -> 46.2 us  [across(): lax.ppermute(pieces, 'member', [(i, member_at(i, 1, 0)) for i in range(SH...]
    all_to_all x3, waiting for transfers between devices: 84.2 us -> 49.5 us  [the longest x2 36.3 us: traded(): lax.all_to_all(pieces, 'member', 0, 0, axis_index_groups=groups, tiled=True)]
    ppermute x1, waiting for transfers between devices: 10.9 us -> 4.73 us  [from_beside(): lax.ppermute(cells, 'region', [((i + 1) % count, i) for i in range(count)])]
    ppermute x1, waiting for transfers between devices: 11.7 us -> 6.6 us  [from_beside(): lax.ppermute(cells, 'region', [(i, (i + 1) % count) for i in range(count)])]
    all_to_all x3, starting transfers between devices: 25.4 us -> 21.8 us  [the longest x2 13.9 us: traded(): lax.all_to_all(pieces, 'member', 0, 0, axis_index_groups=groups, tiled=True)]
    concatenate x0 -> x2, other arithmetic: none -> 3.55 us  [the longest x1 2.9 us: body(): both = jnp.concatenate([near, across(far)], axis=1)]
    pallas_call x5 -> x8, Pallas kernels: 23 us -> 25.6 us  [the longest x2 10.4 us: apply(): pl.pallas_call(apply_kernel, grid=(TILE_POINTS // WIDTH,), in_specs=[pl.B...]
    ppermute x4, waiting for transfers between devices: 3.13 us -> 0.54 us  [sent(): lax.ppermute(piece, 'member', [(i, member_at(i, 0, step)) for i in range(...]
  transfers between devices with their start and end apart: 14 -> 16, of which waited for: 10 -> 12; matrix products, arithmetic and copies ran while one was open for 1% -> 2% of each run, Pallas kernels for 14% -> 16%
where the time goes in v4:
time: 237 us; the launch traced here: 236 us
  waiting for transfers between devices  145 us (61%)
  Pallas kernels  45.6 us (19%)
  starting transfers between devices  39.8 us (17%)
  other arithmetic  3.66 us (2%)
    ppermute x2, waiting for transfers between devices, across(): lax.ppermute(pieces, 'member', [(i, member_at(i, 1, 0)) for i in range(SH...  46.2 us
    ppermute x5, waiting for transfers between devices, from_around(): got.append(lax.ppermute(near, ('region', 'member'), pairs))  37.2 us
    all_to_all x2, waiting for transfers between devices, traded(): lax.all_to_all(pieces, 'member', 0, 0, axis_index_groups=groups, tiled=True)  36.3 us
    pallas_call x1, Pallas kernels, analysis(): pl.pallas_call(functools.partial(analysis_kernel, cycle), grid_spec=pltpu...  20 us
    all_to_all x2, starting transfers between devices, traded(): lax.all_to_all(pieces, 'member', 0, 0, axis_index_groups=groups, tiled=True)  13.9 us
    all_to_all x1, waiting for transfers between devices, traded_by_all(): lax.all_to_all(pieces, 'member', 0, 0, axis_index_groups=[ALL_LISTED], ti...  13.2 us
    ppermute x4, starting transfers between devices, sent(): lax.ppermute(piece, 'member', [(i, member_at(i, 0, step)) for i in range(...  11.9 us
    pallas_call x2, Pallas kernels, apply(): pl.pallas_call(apply_kernel, grid=(TILE_POINTS // WIDTH,), in_specs=[pl.B...  10.4 us
  transfers between devices with their start and end apart: 16, of which 12 were waited for; matrix products, arithmetic and copies ran while one was open for 2% of the time, Pallas kernels for 16%

profile of v4, /device:TPU:46, one launch (start us, length us, event | category | flops | bytes accessed | tf_op | source)
XLA Modules:
  0.0 236.4 jit_solution(850783211610394846)
XLA Ops:
  0.0 6.3 %collective-permute-start = (f32[2,16,256]{2,1,0:T(8,128)}, f32[2,16,256]{2,1,0:T(8,128)S(1)}, u32[]{:S(2)}, u32[]{:S(2)}) collective-permute-start(f32[2,16,256]{2,1,0:T(8,128)} %param.11), channel_id=1, source_target_pairs={{0,4},{1,5},{2,6},{3,7},{4,0},{5,1},{6,2},{7,3},{8,12},{9,13},{10,... | collective-permute-start | bytes 98312 | tf_op jit(solution)/shard_map/ppermute | solution.py:363
  6.3 2.7 %pack.2.refs_0_ = f32[16,2,16,2048]{3,2,1,0:T(8,128)} custom-call(f32[2,16,16,2048]{3,2,1,0:T(8,128)} %x_ref.3), custom_call_target="tpu_custom_call" | custom-call | bytes 4194304 | tf_op jit(solution)/shard_map/pack/pallas_call | solution.py:60
  11.6 3.0 %collective-permute-start.1 = (f32[2,2,16,256]{3,2,1,0:T(8,128)S(1)}, f32[2,2,16,256]{3,2,1,0:T(8,128)S(1)}, u32[]{:S(2)}, u32[]{:S(2)}) collective-permute-start(f32[2,2,16,256]{3,2,1,0:T(8,128)S(1)} %pad_maximum_fusion.1), channel_id=1, source_target_pairs={{0,1},{1,2},{2,3},{3,4},{4,5},{5,6},{6,7},{7,0},{8,9},{9,10},{10,1... | collective-permute-start | bytes 196616 | tf_op jit(solution)/shard_map/ppermute | solution.py:363
  14.6 2.7 %pack.3 = f32[16,2,16,2048]{3,2,1,0:T(8,128)} custom-call(f32[2,16,16,2048]{3,2,1,0:T(8,128)} %x_ref.3, f32[16,2,16,2048]{3,2,1,0:T(8,128)} %pack.2.refs_0_), custom_call_target="tpu_custom_call", output_to_operand_aliasing={{}: (1, {})} | custom-call | bytes 4194304 | tf_op jit(solution)/shard_map/pack/pallas_call | solution.py:60
  18.0 7.8 %all-to-all-start = ((f32[16,2,16,2048]{3,2,1,0:T(8,128)}), f32[16,2,16,2048]{3,2,1,0:T(8,128)}, u32[]{:S(2)}, u32[]{:S(2)}) async-start(f32[16,2,16,2048]{3,2,1,0:T(8,128)} %pack.3), calls=%async_computation | async-start | bytes 8388608 | tf_op jit(solution)/shard_map/all_to_all | solution.py:349
  28.5 2.9 %collective-permute-start.4 = (f32[8,2,16,256]{3,2,1,0:T(8,128)S(1)}, f32[8,2,16,256]{3,2,1,0:T(8,128)S(1)}, u32[]{:S(2)}, u32[]{:S(2)}) collective-permute-start(f32[8,2,16,256]{3,2,1,0:T(8,128)S(1)} %constant_dynamic-update-slice_fusion.own_near), channel_id=1, source_target_pairs={{0,16},{1,17},{2,18},{3,19},{4,20},{5,21},{6,22},{7,23},{8,24},{9,... | collective-permute-start | bytes 786440 | tf_op jit(solution)/shard_map/ppermute | solution.py:388
  31.6 2.9 %collective-permute-done.8.next_far = f32[8,2,16,256]{3,2,1,0:T(8,128)S(1)} collective-permute-done((f32[8,2,16,256]{3,2,1,0:T(8,128)S(1)}, f32[8,2,16,256]{3,2,1,0:T(8,128)S(1)}, u32[]{:S(2)}, u32[]{:S(2)}) %collective-permute-start.8) | collective-permute-done | bytes 262176 | tf_op jit(solution)/shard_map/ppermute | solution.py:388
  34.5 25.4 %collective-permute-done.7.next_near = f32[8,2,16,256]{3,2,1,0:T(8,128)S(1)} collective-permute-done((f32[8,2,16,256]{3,2,1,0:T(8,128)S(1)}, f32[8,2,16,256]{3,2,1,0:T(8,128)S(1)}, u32[]{:S(2)}, u32[]{:S(2)}) %collective-permute-start.7) | collective-permute-done | bytes 262176 | tf_op jit(solution)/shard_map/ppermute | solution.py:388
  59.9 5.6 %collective-permute-done.6.own_far = f32[8,2,16,256]{3,2,1,0:T(8,128)S(1)} collective-permute-done((f32[8,2,16,256]{3,2,1,0:T(8,128)S(1)}, f32[8,2,16,256]{3,2,1,0:T(8,128)S(1)}, u32[]{:S(2)}, u32[]{:S(2)}) %collective-permute-start.6) | collective-permute-done | bytes 262176 | tf_op jit(solution)/shard_map/ppermute | solution.py:388
  65.5 3.3 %collective-permute-done.5.prev_far = f32[8,2,16,256]{3,2,1,0:T(8,128)S(1)} collective-permute-done((f32[8,2,16,256]{3,2,1,0:T(8,128)S(1)}, f32[8,2,16,256]{3,2,1,0:T(8,128)S(1)}, u32[]{:S(2)}, u32[]{:S(2)}) %collective-permute-start.5) | collective-permute-done | bytes 262176 | tf_op jit(solution)/shard_map/ppermute | solution.py:388
  68.8 20.0 %analysis.1.own_ref = f32[264,256]{1,0:T(8,128)S(1)} custom-call(s32[1]{0:T(128)} %bitcast.1.place_ref, s32[32]{0:T(128)S(1)} %copy-done.4, s32[32,4]{1,0:T(8,128)S(1)} %copy.16.nbr_ref, f32[16]{0:T(128)S(1)} %copy-done.1, f32[8,2,16,256]{3,2,1,0:T(8,128)S(1)} %collective-permute-done.4.prev_near, f32[8,2,16,256]{3,2,1,0:T(8,128)S(1)} %collective-permute-done.5.prev_far, ...), custom_call_target="tpu_custom_call" | custom-call | flops 12079595520 | bytes 3145728 | tf_op jit(solution)/shard_map/analysis/pallas_call | solution.py:211
  89.6 4.7 %collective-permute-done.10.next_ref = f32[264,256]{1,0:T(8,128)S(1)} collective-permute-done((f32[264,256]{1,0:T(8,128)S(1)}, f32[264,256]{1,0:T(8,128)S(1)}, u32[]{:S(2)}, u32[]{:S(2)}) %collective-permute-start.10) | collective-permute-done | bytes 270368 | tf_op jit(solution)/shard_map/ppermute | solution.py:395
  94.3 6.6 %collective-permute-done.9.prev_ref = f32[264,256]{1,0:T(8,128)S(1)} collective-permute-done((f32[264,256]{1,0:T(8,128)S(1)}, f32[264,256]{1,0:T(8,128)S(1)}, u32[]{:S(2)}, u32[]{:S(2)}) %collective-permute-start.9) | collective-permute-done | bytes 270368 | tf_op jit(solution)/shard_map/ppermute | solution.py:394
  102.6 13.2 %all-to-all-done.x_ref = f32[16,2,16,2048]{3,2,1,0:T(8,128)} async-done(((f32[16,2,16,2048]{3,2,1,0:T(8,128)}), f32[16,2,16,2048]{3,2,1,0:T(8,128)}, u32[]{:S(2)}, u32[]{:S(2)}) %all-to-all-start) | async-done | bytes 4194336 | tf_op jit(solution)/shard_map/all_to_all | solution.py:349
  115.8 5.2 %apply.3 = f32[8,2,16,2048]{3,2,1,0:T(8,128)} custom-call(f32[2,256,256]{2,1,0:T(8,128)S(1)} %blend.1.mix_ref, f32[16,2,16,2048]{3,2,1,0:T(8,128)} %all-to-all-done.x_ref), custom_call_target="tpu_custom_call" | custom-call | flops 1610612736 | bytes 5242880 | tf_op jit(solution)/shard_map/apply/pallas_call | solution.py:316
  121.0 9.6 %all-to-all-start.1 = ((f32[8,2,16,2048]{3,2,1,0:T(8,128)}), f32[8,2,16,2048]{3,2,1,0:T(8,128)S(1)}, u32[]{:S(2)}, u32[]{:S(2)}) async-start(f32[8,2,16,2048]{3,2,1,0:T(8,128)} %apply.3), calls=%async_computation.1 | async-start | bytes 4194304 | tf_op jit(solution)/shard_map/all_to_all | solution.py:354
  130.6 5.2 %apply.2 = (f32[8,1,16,2048]{3,2,1,0:T(8,128)}, f32[8,1,16,2048]{3,2,1,0:T(8,128)}) custom-call(f32[2,256,256]{2,1,0:T(8,128)S(1)} %blend.1.mix_ref, f32[16,2,16,2048]{3,2,1,0:T(8,128)} %all-to-all-done.x_ref), custom_call_target="tpu_custom_call" | custom-call | flops 1610612736 | bytes 5242880 | tf_op jit(solution)/shard_map/apply/pallas_call | solution.py:316
  135.7 24.7 %collective-permute-done.11 = f32[8,1,16,2048]{3,2,1,0:T(8,128)S(1)} collective-permute-done((f32[8,1,16,2048]{3,2,1,0:T(8,128)}, f32[8,1,16,2048]{3,2,1,0:T(8,128)S(1)}, u32[]{:S(2)}, u32[]{:S(2)}) %collective-permute-start.11) | collective-permute-done | bytes 1048608 | tf_op jit(solution)/shard_map/ppermute | solution.py:358
  160.5 2.9 %pad_maximum_fusion = f32[8,2,16,2048]{3,2,1,0:T(8,128)} fusion(f32[8,1,16,2048]{3,2,1,0:T(8,128)S(1)} %collective-permute-done.11, f32[8,1,16,2048]{3,2,1,0:T(8,128)} %get-tuple-element.21), kind=kLoop, calls=%fused_computation | loop fusion | flops 524288 | bytes 4194304 | tf_op jit(solution)/shard_map/concatenate | solution.py:440
  163.4 16.3 %all-to-all-done.1.x_ref = f32[8,2,16,2048]{3,2,1,0:T(8,128)S(1)} async-done(((f32[8,2,16,2048]{3,2,1,0:T(8,128)}), f32[8,2,16,2048]{3,2,1,0:T(8,128)S(1)}, u32[]{:S(2)}, u32[]{:S(2)}) %all-to-all-start.1) | async-done | bytes 2097184 | tf_op jit(solution)/shard_map/all_to_all | solution.py:354
  179.6 4.4 %all-to-all-start.2 = ((f32[8,2,16,2048]{3,2,1,0:T(8,128)}), f32[8,2,16,2048]{3,2,1,0:T(8,128)}, u32[]{:S(2)}, u32[]{:S(2)}) async-start(f32[8,2,16,2048]{3,2,1,0:T(8,128)} %pad_maximum_fusion), calls=%async_computation.2 | async-start | bytes 4194304 | tf_op jit(solution)/shard_map/all_to_all | solution.py:354
  188.1 21.5 %collective-permute-done.12.x_ref = f32[8,1,16,2048]{3,2,1,0:T(8,128)S(1)} collective-permute-done((f32[8,1,16,2048]{3,2,1,0:T(8,128)}, f32[8,1,16,2048]{3,2,1,0:T(8,128)S(1)}, u32[]{:S(2)}, u32[]{:S(2)}) %collective-permute-start.12) | collective-permute-done | bytes 1048608 | tf_op jit(solution)/shard_map/ppermute | solution.py:358
  213.0 20.0 %all-to-all-done.2.x_ref = f32[8,2,16,2048]{3,2,1,0:T(8,128)} async-done(((f32[8,2,16,2048]{3,2,1,0:T(8,128)}), f32[8,2,16,2048]{3,2,1,0:T(8,128)}, u32[]{:S(2)}, u32[]{:S(2)}) %all-to-all-start.2) | async-done | bytes 2097184 | tf_op jit(solution)/shard_map/all_to_all | solution.py:354
  233.0 3.4 %unpack.5 = f32[2,16,16,2048]{3,2,1,0:T(8,128)} custom-call(s32[2]{0:T(128)} %pad_add_fusion._, f32[8,2,16,2048]{3,2,1,0:T(8,128)} %all-to-all-done.2.x_ref, f32[2,16,16,2048]{3,2,1,0:T(8,128)} %unpack.4.refs_0_), custom_call_target="tpu_custom_call", output_to_operand_aliasing={{}: (2, {})} | custom-call | bytes 4194304 | tf_op jit(solution)/shard_map/unpack/pallas_call | solution.py:83
  (52 shorter events, 15.9 us)
Async XLA Ops:
  0.0 9.0 %collective-permute-start = (f32[2,16,256]{2,1,0:T(8,128)}, f32[2,16,256]{2,1,0:T(8,128)S(1)}, u32[]{:S(2)}, u32[]{:S(2)}) collective-permute-start(f32[2,16,256]{2,1,0:T(8,128)} %param.11), channel_id=1, source_target_pairs={{0,4},{1,5},{2,6},{3,7},{4,0},{5,1},{6,2},{7,3},{8,12},{9,13},{10,... | collective-permute-start | bytes 98312 | tf_op jit(solution)/shard_map/ppermute | solution.py:363
  9.0 8.4 %collective-permute-start.3 = (f32[2,2,16,256]{3,2,1,0:T(8,128)S(1)}, f32[2,2,16,256]{3,2,1,0:T(8,128)S(1)}, u32[]{:S(2)}, u32[]{:S(2)}) collective-permute-start(f32[2,2,16,256]{3,2,1,0:T(8,128)S(1)} %pad_maximum_fusion.1), channel_id=1, source_target_pairs={{0,7},{1,0},{2,1},{3,2},{4,3},{5,4},{6,5},{7,6},{8,15},{9,8},{10,9... | collective-permute-start | bytes 196616 | tf_op jit(solution)/shard_map/ppermute | solution.py:363
  10.1 7.8 %collective-permute-start.2 = (f32[2,2,16,256]{3,2,1,0:T(8,128)S(1)}, f32[2,2,16,256]{3,2,1,0:T(8,128)S(1)}, u32[]{:S(2)}, u32[]{:S(2)}) collective-permute-start(f32[2,2,16,256]{3,2,1,0:T(8,128)S(1)} %pad_maximum_fusion.1), channel_id=1, source_target_pairs={{0,2},{1,3},{2,4},{3,5},{4,6},{5,7},{6,0},{7,1},{8,10},{9,11},{10,... | collective-permute-start | bytes 196616 | tf_op jit(solution)/shard_map/ppermute | solution.py:363
  11.6 6.3 %collective-permute-start.1 = (f32[2,2,16,256]{3,2,1,0:T(8,128)S(1)}, f32[2,2,16,256]{3,2,1,0:T(8,128)S(1)}, u32[]{:S(2)}, u32[]{:S(2)}) collective-permute-start(f32[2,2,16,256]{3,2,1,0:T(8,128)S(1)} %pad_maximum_fusion.1), channel_id=1, source_target_pairs={{0,1},{1,2},{2,3},{3,4},{4,5},{5,6},{6,7},{7,0},{8,9},{9,10},{10,1... | collective-permute-start | bytes 196616 | tf_op jit(solution)/shard_map/ppermute | solution.py:363
  17.4 14.0 %copy-start.9 = (s32[32,4]{0,1:T(4,128)S(1)}, s32[32,4]{0,1:T(4,128)}, u32[]{:S(2)}) copy-start(s32[32,4]{0,1:T(4,128)} %param.15) | copy-start | bytes 1540
  17.4 14.1 %copy-start.7 = (s32[32,5,256]{2,0,1:T(8,128)S(1)}, s32[32,5,256]{2,0,1:T(8,128)}, u32[]{:S(2)}) copy-start(s32[32,5,256]{2,0,1:T(8,128)} %param.16) | copy-start | bytes 491524
  17.4 14.2 %copy-start.10 = (s32[8]{0:T(128)S(1)}, s32[8]{0:T(128)}, u32[]{:S(2)}) copy-start(s32[8]{0:T(128)} %constant.50) | copy-start | bytes 100
  17.4 51.4 %copy-start.1 = (f32[16]{0:T(128)S(1)}, f32[16]{0:T(128)}, u32[]{:S(2)}) copy-start(f32[16]{0:T(128)} %factor_ref.3) | copy-start | bytes 196
  17.4 51.4 %copy-start.2 = (f32[32,256]{1,0:T(8,128)S(1)}, f32[32,256]{1,0:T(8,128)}, u32[]{:S(2)}) copy-start(f32[32,256]{1,0:T(8,128)} %values_ref.1) | copy-start | bytes 98308
  17.4 51.4 %copy-start.3 = (f32[32,256]{1,0:T(8,128)S(1)}, f32[32,256]{1,0:T(8,128)}, u32[]{:S(2)}) copy-start(f32[32,256]{1,0:T(8,128)} %precision_ref.1) | copy-start | bytes 98308
  17.4 51.4 %copy-start.4 = (s32[32]{0:T(128)S(1)}, s32[32]{0:T(128)}, u32[]{:S(2)}) copy-start(s32[32]{0:T(128)} %live_ref.1) | copy-start | bytes 388
  18.0 97.8 %all-to-all-start = ((f32[16,2,16,2048]{3,2,1,0:T(8,128)}), f32[16,2,16,2048]{3,2,1,0:T(8,128)}, u32[]{:S(2)}, u32[]{:S(2)}) async-start(f32[16,2,16,2048]{3,2,1,0:T(8,128)} %pack.3), calls=%async_computation | async-start | bytes 8388608 | tf_op jit(solution)/shard_map/all_to_all | solution.py:349
  25.8 8.7 %collective-permute-start.8 = (f32[8,2,16,256]{3,2,1,0:T(8,128)S(1)}, f32[8,2,16,256]{3,2,1,0:T(8,128)S(1)}, u32[]{:S(2)}, u32[]{:S(2)}) collective-permute-start(f32[8,2,16,256]{3,2,1,0:T(8,128)S(1)} %constant_dynamic-update-slice_fusion.own_near), channel_id=1, source_target_pairs={{0,248},{1,249},{2,250},{3,251},{4,252},{5,253},{6,254},{7,255},{8... | collective-permute-start | bytes 786440 | tf_op jit(solution)/shard_map/ppermute | solution.py:388
  25.9 34.0 %collective-permute-start.7 = (f32[8,2,16,256]{3,2,1,0:T(8,128)S(1)}, f32[8,2,16,256]{3,2,1,0:T(8,128)S(1)}, u32[]{:S(2)}, u32[]{:S(2)}) collective-permute-start(f32[8,2,16,256]{3,2,1,0:T(8,128)S(1)} %constant_dynamic-update-slice_fusion.own_near), channel_id=1, source_target_pairs={{0,240},{1,241},{2,242},{3,243},{4,244},{5,245},{6,246},{7,247},{8... | collective-permute-start | bytes 786440 | tf_op jit(solution)/shard_map/ppermute | solution.py:388
  27.6 37.9 %collective-permute-start.6 = (f32[8,2,16,256]{3,2,1,0:T(8,128)S(1)}, f32[8,2,16,256]{3,2,1,0:T(8,128)S(1)}, u32[]{:S(2)}, u32[]{:S(2)}) collective-permute-start(f32[8,2,16,256]{3,2,1,0:T(8,128)S(1)} %constant_dynamic-update-slice_fusion.own_near), channel_id=1, source_target_pairs={{0,8},{1,9},{2,10},{3,11},{4,12},{5,13},{6,14},{7,15},{8,0},{9,1},... | collective-permute-start | bytes 786440 | tf_op jit(solution)/shard_map/ppermute | solution.py:388
  28.5 40.3 %collective-permute-start.5 = (f32[8,2,16,256]{3,2,1,0:T(8,128)S(1)}, f32[8,2,16,256]{3,2,1,0:T(8,128)S(1)}, u32[]{:S(2)}, u32[]{:S(2)}) collective-permute-start(f32[8,2,16,256]{3,2,1,0:T(8,128)S(1)} %constant_dynamic-update-slice_fusion.own_near), channel_id=1, source_target_pairs={{0,24},{1,25},{2,26},{3,27},{4,28},{5,29},{6,30},{7,31},{8,16},{9,... | collective-permute-start | bytes 786440 | tf_op jit(solution)/shard_map/ppermute | solution.py:388
  28.5 40.3 %collective-permute-start.4 = (f32[8,2,16,256]{3,2,1,0:T(8,128)S(1)}, f32[8,2,16,256]{3,2,1,0:T(8,128)S(1)}, u32[]{:S(2)}, u32[]{:S(2)}) collective-permute-start(f32[8,2,16,256]{3,2,1,0:T(8,128)S(1)} %constant_dynamic-update-slice_fusion.own_near), channel_id=1, source_target_pairs={{0,16},{1,17},{2,18},{3,19},{4,20},{5,21},{6,22},{7,23},{8,24},{9,... | collective-permute-start | bytes 786440 | tf_op jit(solution)/shard_map/ppermute | solution.py:388
  68.8 32.1 %copy-start = (s32[2,1,5]{2,1,0:T(1,128)S(1)}, s32[2,1,5]{2,1,0:T(1,128)}, u32[]{:S(2)}) copy-start(s32[2,1,5]{2,1,0:T(1,128)} %blend_ref.1) | copy-start | bytes 124
  88.9 5.5 %collective-permute-start.10 = (f32[264,256]{1,0:T(8,128)S(1)}, f32[264,256]{1,0:T(8,128)S(1)}, u32[]{:S(2)}, u32[]{:S(2)}) collective-permute-start(f32[264,256]{1,0:T(8,128)S(1)} %analysis.1.own_ref), channel_id=1, source_target_pairs={{16,0},{32,16},{48,32},{64,48},{80,64},{96,80},{112,96},{128,112},... | collective-permute-start | bytes 811016 | tf_op jit(solution)/shard_map/ppermute | solution.py:395
  89.5 11.4 %collective-permute-start.9 = (f32[264,256]{1,0:T(8,128)S(1)}, f32[264,256]{1,0:T(8,128)S(1)}, u32[]{:S(2)}, u32[]{:S(2)}) collective-permute-start(f32[264,256]{1,0:T(8,128)S(1)} %analysis.1.own_ref), channel_id=1, source_target_pairs={{0,16},{16,32},{32,48},{48,64},{64,80},{80,96},{96,112},{112,128},... | collective-permute-start | bytes 811016 | tf_op jit(solution)/shard_map/ppermute | solution.py:394
  121.0 58.7 %all-to-all-start.1 = ((f32[8,2,16,2048]{3,2,1,0:T(8,128)}), f32[8,2,16,2048]{3,2,1,0:T(8,128)S(1)}, u32[]{:S(2)}, u32[]{:S(2)}) async-start(f32[8,2,16,2048]{3,2,1,0:T(8,128)} %apply.3), calls=%async_computation.1 | async-start | bytes 4194304 | tf_op jit(solution)/shard_map/all_to_all | solution.py:354
  135.7 24.7 %collective-permute-start.11 = (f32[8,1,16,2048]{3,2,1,0:T(8,128)}, f32[8,1,16,2048]{3,2,1,0:T(8,128)S(1)}, u32[]{:S(2)}, u32[]{:S(2)}) collective-permute-start(f32[8,1,16,2048]{3,2,1,0:T(8,128)} %get-tuple-element.22), channel_id=1, source_target_pairs={{0,8},{1,9},{2,10},{3,11},{4,12},{5,13},{6,14},{7,15},{8,0},{9,1},... | collective-permute-start | bytes 3145736 | tf_op jit(solution)/shard_map/ppermute | solution.py:358
  179.6 53.3 %all-to-all-start.2 = ((f32[8,2,16,2048]{3,2,1,0:T(8,128)}), f32[8,2,16,2048]{3,2,1,0:T(8,128)}, u32[]{:S(2)}, u32[]{:S(2)}) async-start(f32[8,2,16,2048]{3,2,1,0:T(8,128)} %pad_maximum_fusion), calls=%async_computation.2 | async-start | bytes 4194304 | tf_op jit(solution)/shard_map/all_to_all | solution.py:354
  185.0 24.5 %collective-permute-start.12 = (f32[8,1,16,2048]{3,2,1,0:T(8,128)}, f32[8,1,16,2048]{3,2,1,0:T(8,128)S(1)}, u32[]{:S(2)}, u32[]{:S(2)}) collective-permute-start(f32[8,1,16,2048]{3,2,1,0:T(8,128)} %slice.3), channel_id=1, source_target_pairs={{0,8},{1,9},{2,10},{3,11},{4,12},{5,13},{6,14},{7,15},{8,0},{9,1},... | collective-permute-start | bytes 3145736 | tf_op jit(solution)/shard_map/ppermute | solution.py:358
  (3 other events, 16.1 us)

commit v5 on v4

--- a/solution.py
+++ b/solution.py
@@ -38,8 +38,8 @@
 WIDTH = 512
 SIDES = SHARES // RINGS
 
-LISTED = [0, 2, 5, 1, 7, 4, 3, 6]
-ALL_LISTED = [0, 7, 1, 6, 2, 5, 3, 4, 12, 11, 13, 10, 14, 9, 15, 8]
+LISTED = [0, 4, 1, 5, 2, 6, 3, 7]
+ALL_LISTED = [0, 3, 6, 1, 4, 7, 2, 5, 8, 11, 14, 9, 12, 15, 10, 13]
 HALF = SHARE // 2
 
 

time: 237 us -> 234 us (0.987)
  waiting for transfers between devices: 145 us -> 141 us
    all_to_all x2, starting transfers between devices: 13.9 us -> 9.91 us  [traded(): lax.all_to_all(pieces, 'member', 0, 0, axis_index_groups=groups, tiled=True)]
    all_to_all x1, waiting for transfers between devices: 13.2 us -> 9.56 us  [traded_by_all(): lax.all_to_all(pieces, 'member', 0, 0, axis_index_groups=[ALL_LISTED], ti...]
    ppermute x1, waiting for transfers between devices: 4.73 us -> 7.35 us  [from_beside(): lax.ppermute(cells, 'region', [((i + 1) % count, i) for i in range(count)])]
    ppermute x2, starting transfers between devices: 0.01 us -> 2.55 us  [across(): lax.ppermute(pieces, 'member', [(i, member_at(i, 1, 0)) for i in range(SH...]
    ppermute x2, waiting for transfers between devices: 46.2 us -> 43.8 us  [across(): lax.ppermute(pieces, 'member', [(i, member_at(i, 1, 0)) for i in range(SH...]
where the time goes in v5:
time: 234 us; the launch traced here: 232 us
  waiting for transfers between devices  141 us (60%)
  Pallas kernels  45.6 us (19%)
  starting transfers between devices  40.1 us (17%)
  other arithmetic  3.66 us (2%)
    ppermute x2, waiting for transfers between devices, across(): lax.ppermute(pieces, 'member', [(i, member_at(i, 1, 0)) for i in range(SH...  43.8 us
    ppermute x5, waiting for transfers between devices, from_around(): got.append(lax.ppermute(near, ('region', 'member'), pairs))  38.3 us
    all_to_all x2, waiting for transfers between devices, traded(): lax.all_to_all(pieces, 'member', 0, 0, axis_index_groups=groups, tiled=True)  35.2 us
    pallas_call x1, Pallas kernels, analysis(): pl.pallas_call(functools.partial(analysis_kernel, cycle), grid_spec=pltpu...  20 us
    ppermute x4, starting transfers between devices, sent(): lax.ppermute(piece, 'member', [(i, member_at(i, 0, step)) for i in range(...  11.9 us
    pallas_call x2, Pallas kernels, apply(): pl.pallas_call(apply_kernel, grid=(TILE_POINTS // WIDTH,), in_specs=[pl.B...  10.4 us
    all_to_all x2, starting transfers between devices, traded(): lax.all_to_all(pieces, 'member', 0, 0, axis_index_groups=groups, tiled=True)  9.91 us
    all_to_all x1, waiting for transfers between devices, traded_by_all(): lax.all_to_all(pieces, 'member', 0, 0, axis_index_groups=[ALL_LISTED], ti...  9.56 us
  transfers between devices with their start and end apart: 16, of which 12 were waited for; matrix products, arithmetic and copies ran while one was open for 2% of the time, Pallas kernels for 16%

profile of v5, /device:TPU:46, one launch (start us, length us, event | category | flops | bytes accessed | tf_op | source)
XLA Modules:
  0.0 232.4 jit_solution(8282223146069868405)
XLA Ops:
  0.0 6.3 %collective-permute-start = (f32[2,16,256]{2,1,0:T(8,128)}, f32[2,16,256]{2,1,0:T(8,128)S(1)}, u32[]{:S(2)}, u32[]{:S(2)}) collective-permute-start(f32[2,16,256]{2,1,0:T(8,128)} %param.11), channel_id=1, source_target_pairs={{0,4},{1,5},{2,6},{3,7},{4,0},{5,1},{6,2},{7,3},{8,12},{9,13},{10,... | collective-permute-start | bytes 98312 | tf_op jit(solution)/shard_map/ppermute | solution.py:363
  6.3 2.7 %pack.2.refs_0_ = f32[16,2,16,2048]{3,2,1,0:T(8,128)} custom-call(f32[2,16,16,2048]{3,2,1,0:T(8,128)} %x_ref.3), custom_call_target="tpu_custom_call" | custom-call | bytes 4194304 | tf_op jit(solution)/shard_map/pack/pallas_call | solution.py:60
  11.6 3.0 %collective-permute-start.1 = (f32[2,2,16,256]{3,2,1,0:T(8,128)S(1)}, f32[2,2,16,256]{3,2,1,0:T(8,128)S(1)}, u32[]{:S(2)}, u32[]{:S(2)}) collective-permute-start(f32[2,2,16,256]{3,2,1,0:T(8,128)S(1)} %pad_maximum_fusion.1), channel_id=1, source_target_pairs={{0,1},{1,2},{2,3},{3,4},{4,5},{5,6},{6,7},{7,0},{8,9},{9,10},{10,1... | collective-permute-start | bytes 196616 | tf_op jit(solution)/shard_map/ppermute | solution.py:363
  14.6 2.7 %pack.3 = f32[16,2,16,2048]{3,2,1,0:T(8,128)} custom-call(f32[2,16,16,2048]{3,2,1,0:T(8,128)} %x_ref.3, f32[16,2,16,2048]{3,2,1,0:T(8,128)} %pack.2.refs_0_), custom_call_target="tpu_custom_call", output_to_operand_aliasing={{}: (1, {})} | custom-call | bytes 4194304 | tf_op jit(solution)/shard_map/pack/pallas_call | solution.py:60
  18.0 7.8 %all-to-all-start = ((f32[16,2,16,2048]{3,2,1,0:T(8,128)}), f32[16,2,16,2048]{3,2,1,0:T(8,128)}, u32[]{:S(2)}, u32[]{:S(2)}) async-start(f32[16,2,16,2048]{3,2,1,0:T(8,128)} %pack.3), calls=%async_computation | async-start | bytes 8388608 | tf_op jit(solution)/shard_map/all_to_all | solution.py:349
  28.5 2.9 %collective-permute-start.4 = (f32[8,2,16,256]{3,2,1,0:T(8,128)S(1)}, f32[8,2,16,256]{3,2,1,0:T(8,128)S(1)}, u32[]{:S(2)}, u32[]{:S(2)}) collective-permute-start(f32[8,2,16,256]{3,2,1,0:T(8,128)S(1)} %constant_dynamic-update-slice_fusion.own_near), channel_id=1, source_target_pairs={{0,16},{1,17},{2,18},{3,19},{4,20},{5,21},{6,22},{7,23},{8,24},{9,... | collective-permute-start | bytes 786440 | tf_op jit(solution)/shard_map/ppermute | solution.py:388
  31.6 19.2 %collective-permute-done.8.next_far = f32[8,2,16,256]{3,2,1,0:T(8,128)S(1)} collective-permute-done((f32[8,2,16,256]{3,2,1,0:T(8,128)S(1)}, f32[8,2,16,256]{3,2,1,0:T(8,128)S(1)}, u32[]{:S(2)}, u32[]{:S(2)}) %collective-permute-start.8) | collective-permute-done | bytes 262176 | tf_op jit(solution)/shard_map/ppermute | solution.py:388
  50.8 3.9 %collective-permute-done.7.next_near = f32[8,2,16,256]{3,2,1,0:T(8,128)S(1)} collective-permute-done((f32[8,2,16,256]{3,2,1,0:T(8,128)S(1)}, f32[8,2,16,256]{3,2,1,0:T(8,128)S(1)}, u32[]{:S(2)}, u32[]{:S(2)}) %collective-permute-start.7) | collective-permute-done | bytes 262176 | tf_op jit(solution)/shard_map/ppermute | solution.py:388
  54.7 11.1 %collective-permute-done.6.own_far = f32[8,2,16,256]{3,2,1,0:T(8,128)S(1)} collective-permute-done((f32[8,2,16,256]{3,2,1,0:T(8,128)S(1)}, f32[8,2,16,256]{3,2,1,0:T(8,128)S(1)}, u32[]{:S(2)}, u32[]{:S(2)}) %collective-permute-start.6) | collective-permute-done | bytes 262176 | tf_op jit(solution)/shard_map/ppermute | solution.py:388
  65.8 4.1 %collective-permute-done.5.prev_far = f32[8,2,16,256]{3,2,1,0:T(8,128)S(1)} collective-permute-done((f32[8,2,16,256]{3,2,1,0:T(8,128)S(1)}, f32[8,2,16,256]{3,2,1,0:T(8,128)S(1)}, u32[]{:S(2)}, u32[]{:S(2)}) %collective-permute-start.5) | collective-permute-done | bytes 262176 | tf_op jit(solution)/shard_map/ppermute | solution.py:388
  70.0 20.0 %analysis.1.own_ref = f32[264,256]{1,0:T(8,128)S(1)} custom-call(s32[1]{0:T(128)} %bitcast.1.place_ref, s32[32]{0:T(128)S(1)} %copy-done.4, s32[32,4]{1,0:T(8,128)S(1)} %copy.16.nbr_ref, f32[16]{0:T(128)S(1)} %copy-done.1, f32[8,2,16,256]{3,2,1,0:T(8,128)S(1)} %collective-permute-done.4.prev_near, f32[8,2,16,256]{3,2,1,0:T(8,128)S(1)} %collective-permute-done.5.prev_far, ...), custom_call_target="tpu_custom_call" | custom-call | flops 12079595520 | bytes 3145728 | tf_op jit(solution)/shard_map/analysis/pallas_call | solution.py:211
  92.5 7.3 %collective-permute-done.10.next_ref = f32[264,256]{1,0:T(8,128)S(1)} collective-permute-done((f32[264,256]{1,0:T(8,128)S(1)}, f32[264,256]{1,0:T(8,128)S(1)}, u32[]{:S(2)}, u32[]{:S(2)}) %collective-permute-start.10) | collective-permute-done | bytes 270368 | tf_op jit(solution)/shard_map/ppermute | solution.py:395
  99.8 5.7 %collective-permute-done.9.prev_ref = f32[264,256]{1,0:T(8,128)S(1)} collective-permute-done((f32[264,256]{1,0:T(8,128)S(1)}, f32[264,256]{1,0:T(8,128)S(1)}, u32[]{:S(2)}, u32[]{:S(2)}) %collective-permute-start.9) | collective-permute-done | bytes 270368 | tf_op jit(solution)/shard_map/ppermute | solution.py:394
  107.2 9.6 %all-to-all-done.x_ref = f32[16,2,16,2048]{3,2,1,0:T(8,128)} async-done(((f32[16,2,16,2048]{3,2,1,0:T(8,128)}), f32[16,2,16,2048]{3,2,1,0:T(8,128)}, u32[]{:S(2)}, u32[]{:S(2)}) %all-to-all-start) | async-done | bytes 4194336 | tf_op jit(solution)/shard_map/all_to_all | solution.py:349
  116.8 5.2 %apply.3 = f32[8,2,16,2048]{3,2,1,0:T(8,128)} custom-call(f32[2,256,256]{2,1,0:T(8,128)S(1)} %blend.1.mix_ref, f32[16,2,16,2048]{3,2,1,0:T(8,128)} %all-to-all-done.x_ref), custom_call_target="tpu_custom_call" | custom-call | flops 1610612736 | bytes 5242880 | tf_op jit(solution)/shard_map/apply/pallas_call | solution.py:316
  122.0 5.6 %all-to-all-start.1 = ((f32[8,2,16,2048]{3,2,1,0:T(8,128)}), f32[8,2,16,2048]{3,2,1,0:T(8,128)S(1)}, u32[]{:S(2)}, u32[]{:S(2)}) async-start(f32[8,2,16,2048]{3,2,1,0:T(8,128)} %apply.3), calls=%async_computation.1 | async-start | bytes 4194304 | tf_op jit(solution)/shard_map/all_to_all | solution.py:354
  127.6 5.2 %apply.2 = (f32[8,1,16,2048]{3,2,1,0:T(8,128)}, f32[8,1,16,2048]{3,2,1,0:T(8,128)}) custom-call(f32[2,256,256]{2,1,0:T(8,128)S(1)} %blend.1.mix_ref, f32[16,2,16,2048]{3,2,1,0:T(8,128)} %all-to-all-done.x_ref), custom_call_target="tpu_custom_call" | custom-call | flops 1610612736 | bytes 5242880 | tf_op jit(solution)/shard_map/apply/pallas_call | solution.py:316
  134.2 22.7 %collective-permute-done.11 = f32[8,1,16,2048]{3,2,1,0:T(8,128)S(1)} collective-permute-done((f32[8,1,16,2048]{3,2,1,0:T(8,128)}, f32[8,1,16,2048]{3,2,1,0:T(8,128)S(1)}, u32[]{:S(2)}, u32[]{:S(2)}) %collective-permute-start.11) | collective-permute-done | bytes 1048608 | tf_op jit(solution)/shard_map/ppermute | solution.py:358
  156.9 2.9 %pad_maximum_fusion = f32[8,2,16,2048]{3,2,1,0:T(8,128)} fusion(f32[8,1,16,2048]{3,2,1,0:T(8,128)S(1)} %collective-permute-done.11, f32[8,1,16,2048]{3,2,1,0:T(8,128)} %get-tuple-element.21), kind=kLoop, calls=%fused_computation | loop fusion | flops 524288 | bytes 4194304 | tf_op jit(solution)/shard_map/concatenate | solution.py:440
  159.8 16.4 %all-to-all-done.1.x_ref = f32[8,2,16,2048]{3,2,1,0:T(8,128)S(1)} async-done(((f32[8,2,16,2048]{3,2,1,0:T(8,128)}), f32[8,2,16,2048]{3,2,1,0:T(8,128)S(1)}, u32[]{:S(2)}, u32[]{:S(2)}) %all-to-all-start.1) | async-done | bytes 2097184 | tf_op jit(solution)/shard_map/all_to_all | solution.py:354
  176.2 4.3 %all-to-all-start.2 = ((f32[8,2,16,2048]{3,2,1,0:T(8,128)}), f32[8,2,16,2048]{3,2,1,0:T(8,128)}, u32[]{:S(2)}, u32[]{:S(2)}) async-start(f32[8,2,16,2048]{3,2,1,0:T(8,128)} %pad_maximum_fusion), calls=%async_computation.2 | async-start | bytes 4194304 | tf_op jit(solution)/shard_map/all_to_all | solution.py:354
  185.7 21.2 %collective-permute-done.12.x_ref = f32[8,1,16,2048]{3,2,1,0:T(8,128)S(1)} collective-permute-done((f32[8,1,16,2048]{3,2,1,0:T(8,128)}, f32[8,1,16,2048]{3,2,1,0:T(8,128)S(1)}, u32[]{:S(2)}, u32[]{:S(2)}) %collective-permute-start.12) | collective-permute-done | bytes 1048608 | tf_op jit(solution)/shard_map/ppermute | solution.py:358
  210.2 18.7 %all-to-all-done.2.x_ref = f32[8,2,16,2048]{3,2,1,0:T(8,128)} async-done(((f32[8,2,16,2048]{3,2,1,0:T(8,128)}), f32[8,2,16,2048]{3,2,1,0:T(8,128)}, u32[]{:S(2)}, u32[]{:S(2)}) %all-to-all-start.2) | async-done | bytes 2097184 | tf_op jit(solution)/shard_map/all_to_all | solution.py:354
  229.0 3.4 %unpack.5 = f32[2,16,16,2048]{3,2,1,0:T(8,128)} custom-call(s32[2]{0:T(128)} %pad_add_fusion._, f32[8,2,16,2048]{3,2,1,0:T(8,128)} %all-to-all-done.2.x_ref, f32[2,16,16,2048]{3,2,1,0:T(8,128)} %unpack.4.refs_0_), custom_call_target="tpu_custom_call", output_to_operand_aliasing={{}: (2, {})} | custom-call | bytes 4194304 | tf_op jit(solution)/shard_map/unpack/pallas_call | solution.py:83
  (52 shorter events, 20.1 us)
Async XLA Ops:
  0.0 9.0 %collective-permute-start = (f32[2,16,256]{2,1,0:T(8,128)}, f32[2,16,256]{2,1,0:T(8,128)S(1)}, u32[]{:S(2)}, u32[]{:S(2)}) collective-permute-start(f32[2,16,256]{2,1,0:T(8,128)} %param.11), channel_id=1, source_target_pairs={{0,4},{1,5},{2,6},{3,7},{4,0},{5,1},{6,2},{7,3},{8,12},{9,13},{10,... | collective-permute-start | bytes 98312 | tf_op jit(solution)/shard_map/ppermute | solution.py:363
  9.0 8.4 %collective-permute-start.3 = (f32[2,2,16,256]{3,2,1,0:T(8,128)S(1)}, f32[2,2,16,256]{3,2,1,0:T(8,128)S(1)}, u32[]{:S(2)}, u32[]{:S(2)}) collective-permute-start(f32[2,2,16,256]{3,2,1,0:T(8,128)S(1)} %pad_maximum_fusion.1), channel_id=1, source_target_pairs={{0,7},{1,0},{2,1},{3,2},{4,3},{5,4},{6,5},{7,6},{8,15},{9,8},{10,9... | collective-permute-start | bytes 196616 | tf_op jit(solution)/shard_map/ppermute | solution.py:363
  10.1 7.8 %collective-permute-start.2 = (f32[2,2,16,256]{3,2,1,0:T(8,128)S(1)}, f32[2,2,16,256]{3,2,1,0:T(8,128)S(1)}, u32[]{:S(2)}, u32[]{:S(2)}) collective-permute-start(f32[2,2,16,256]{3,2,1,0:T(8,128)S(1)} %pad_maximum_fusion.1), channel_id=1, source_target_pairs={{0,2},{1,3},{2,4},{3,5},{4,6},{5,7},{6,0},{7,1},{8,10},{9,11},{10,... | collective-permute-start | bytes 196616 | tf_op jit(solution)/shard_map/ppermute | solution.py:363
  11.6 6.3 %collective-permute-start.1 = (f32[2,2,16,256]{3,2,1,0:T(8,128)S(1)}, f32[2,2,16,256]{3,2,1,0:T(8,128)S(1)}, u32[]{:S(2)}, u32[]{:S(2)}) collective-permute-start(f32[2,2,16,256]{3,2,1,0:T(8,128)S(1)} %pad_maximum_fusion.1), channel_id=1, source_target_pairs={{0,1},{1,2},{2,3},{3,4},{4,5},{5,6},{6,7},{7,0},{8,9},{9,10},{10,1... | collective-permute-start | bytes 196616 | tf_op jit(solution)/shard_map/ppermute | solution.py:363
  17.4 14.0 %copy-start.9 = (s32[32,4]{0,1:T(4,128)S(1)}, s32[32,4]{0,1:T(4,128)}, u32[]{:S(2)}) copy-start(s32[32,4]{0,1:T(4,128)} %param.15) | copy-start | bytes 1540
  17.4 14.1 %copy-start.7 = (s32[32,5,256]{2,0,1:T(8,128)S(1)}, s32[32,5,256]{2,0,1:T(8,128)}, u32[]{:S(2)}) copy-start(s32[32,5,256]{2,0,1:T(8,128)} %param.16) | copy-start | bytes 491524
  17.4 14.2 %copy-start.10 = (s32[8]{0:T(128)S(1)}, s32[8]{0:T(128)}, u32[]{:S(2)}) copy-start(s32[8]{0:T(128)} %constant.50) | copy-start | bytes 100
  17.4 52.6 %copy-start.1 = (f32[16]{0:T(128)S(1)}, f32[16]{0:T(128)}, u32[]{:S(2)}) copy-start(f32[16]{0:T(128)} %factor_ref.3) | copy-start | bytes 196
  17.4 52.6 %copy-start.2 = (f32[32,256]{1,0:T(8,128)S(1)}, f32[32,256]{1,0:T(8,128)}, u32[]{:S(2)}) copy-start(f32[32,256]{1,0:T(8,128)} %values_ref.1) | copy-start | bytes 98308
  17.4 52.6 %copy-start.3 = (f32[32,256]{1,0:T(8,128)S(1)}, f32[32,256]{1,0:T(8,128)}, u32[]{:S(2)}) copy-start(f32[32,256]{1,0:T(8,128)} %precision_ref.1) | copy-start | bytes 98308
  17.4 52.6 %copy-start.4 = (s32[32]{0:T(128)S(1)}, s32[32]{0:T(128)}, u32[]{:S(2)}) copy-start(s32[32]{0:T(128)} %live_ref.1) | copy-start | bytes 388
  18.0 98.8 %all-to-all-start = ((f32[16,2,16,2048]{3,2,1,0:T(8,128)}), f32[16,2,16,2048]{3,2,1,0:T(8,128)}, u32[]{:S(2)}, u32[]{:S(2)}) async-start(f32[16,2,16,2048]{3,2,1,0:T(8,128)} %pack.3), calls=%async_computation | async-start | bytes 8388608 | tf_op jit(solution)/shard_map/all_to_all | solution.py:349
  25.8 25.0 %collective-permute-start.8 = (f32[8,2,16,256]{3,2,1,0:T(8,128)S(1)}, f32[8,2,16,256]{3,2,1,0:T(8,128)S(1)}, u32[]{:S(2)}, u32[]{:S(2)}) collective-permute-start(f32[8,2,16,256]{3,2,1,0:T(8,128)S(1)} %constant_dynamic-update-slice_fusion.own_near), channel_id=1, source_target_pairs={{0,248},{1,249},{2,250},{3,251},{4,252},{5,253},{6,254},{7,255},{8... | collective-permute-start | bytes 786440 | tf_op jit(solution)/shard_map/ppermute | solution.py:388
  25.9 28.8 %collective-permute-start.7 = (f32[8,2,16,256]{3,2,1,0:T(8,128)S(1)}, f32[8,2,16,256]{3,2,1,0:T(8,128)S(1)}, u32[]{:S(2)}, u32[]{:S(2)}) collective-permute-start(f32[8,2,16,256]{3,2,1,0:T(8,128)S(1)} %constant_dynamic-update-slice_fusion.own_near), channel_id=1, source_target_pairs={{0,240},{1,241},{2,242},{3,243},{4,244},{5,245},{6,246},{7,247},{8... | collective-permute-start | bytes 786440 | tf_op jit(solution)/shard_map/ppermute | solution.py:388
  27.6 38.2 %collective-permute-start.6 = (f32[8,2,16,256]{3,2,1,0:T(8,128)S(1)}, f32[8,2,16,256]{3,2,1,0:T(8,128)S(1)}, u32[]{:S(2)}, u32[]{:S(2)}) collective-permute-start(f32[8,2,16,256]{3,2,1,0:T(8,128)S(1)} %constant_dynamic-update-slice_fusion.own_near), channel_id=1, source_target_pairs={{0,8},{1,9},{2,10},{3,11},{4,12},{5,13},{6,14},{7,15},{8,0},{9,1},... | collective-permute-start | bytes 786440 | tf_op jit(solution)/shard_map/ppermute | solution.py:388
  28.5 41.5 %collective-permute-start.5 = (f32[8,2,16,256]{3,2,1,0:T(8,128)S(1)}, f32[8,2,16,256]{3,2,1,0:T(8,128)S(1)}, u32[]{:S(2)}, u32[]{:S(2)}) collective-permute-start(f32[8,2,16,256]{3,2,1,0:T(8,128)S(1)} %constant_dynamic-update-slice_fusion.own_near), channel_id=1, source_target_pairs={{0,24},{1,25},{2,26},{3,27},{4,28},{5,29},{6,30},{7,31},{8,16},{9,... | collective-permute-start | bytes 786440 | tf_op jit(solution)/shard_map/ppermute | solution.py:388
  28.5 41.5 %collective-permute-start.4 = (f32[8,2,16,256]{3,2,1,0:T(8,128)S(1)}, f32[8,2,16,256]{3,2,1,0:T(8,128)S(1)}, u32[]{:S(2)}, u32[]{:S(2)}) collective-permute-start(f32[8,2,16,256]{3,2,1,0:T(8,128)S(1)} %constant_dynamic-update-slice_fusion.own_near), channel_id=1, source_target_pairs={{0,16},{1,17},{2,18},{3,19},{4,20},{5,21},{6,22},{7,23},{8,24},{9,... | collective-permute-start | bytes 786440 | tf_op jit(solution)/shard_map/ppermute | solution.py:388
  70.0 35.6 %copy-start = (s32[2,1,5]{2,1,0:T(1,128)S(1)}, s32[2,1,5]{2,1,0:T(1,128)}, u32[]{:S(2)}) copy-start(s32[2,1,5]{2,1,0:T(1,128)} %blend_ref.1) | copy-start | bytes 124
  90.0 9.8 %collective-permute-start.10 = (f32[264,256]{1,0:T(8,128)S(1)}, f32[264,256]{1,0:T(8,128)S(1)}, u32[]{:S(2)}, u32[]{:S(2)}) collective-permute-start(f32[264,256]{1,0:T(8,128)S(1)} %analysis.1.own_ref), channel_id=1, source_target_pairs={{16,0},{32,16},{48,32},{64,48},{80,64},{96,80},{112,96},{128,112},... | collective-permute-start | bytes 811016 | tf_op jit(solution)/shard_map/ppermute | solution.py:395
  92.4 13.2 %collective-permute-start.9 = (f32[264,256]{1,0:T(8,128)S(1)}, f32[264,256]{1,0:T(8,128)S(1)}, u32[]{:S(2)}, u32[]{:S(2)}) collective-permute-start(f32[264,256]{1,0:T(8,128)S(1)} %analysis.1.own_ref), channel_id=1, source_target_pairs={{0,16},{16,32},{32,48},{48,64},{64,80},{80,96},{96,112},{112,128},... | collective-permute-start | bytes 811016 | tf_op jit(solution)/shard_map/ppermute | solution.py:394
  122.0 54.2 %all-to-all-start.1 = ((f32[8,2,16,2048]{3,2,1,0:T(8,128)}), f32[8,2,16,2048]{3,2,1,0:T(8,128)S(1)}, u32[]{:S(2)}, u32[]{:S(2)}) async-start(f32[8,2,16,2048]{3,2,1,0:T(8,128)} %apply.3), calls=%async_computation.1 | async-start | bytes 4194304 | tf_op jit(solution)/shard_map/all_to_all | solution.py:354
  132.8 24.1 %collective-permute-start.11 = (f32[8,1,16,2048]{3,2,1,0:T(8,128)}, f32[8,1,16,2048]{3,2,1,0:T(8,128)S(1)}, u32[]{:S(2)}, u32[]{:S(2)}) collective-permute-start(f32[8,1,16,2048]{3,2,1,0:T(8,128)} %get-tuple-element.22), channel_id=1, source_target_pairs={{0,8},{1,9},{2,10},{3,11},{4,12},{5,13},{6,14},{7,15},{8,0},{9,1},... | collective-permute-start | bytes 3145736 | tf_op jit(solution)/shard_map/ppermute | solution.py:358
  176.2 52.8 %all-to-all-start.2 = ((f32[8,2,16,2048]{3,2,1,0:T(8,128)}), f32[8,2,16,2048]{3,2,1,0:T(8,128)}, u32[]{:S(2)}, u32[]{:S(2)}) async-start(f32[8,2,16,2048]{3,2,1,0:T(8,128)} %pad_maximum_fusion), calls=%async_computation.2 | async-start | bytes 4194304 | tf_op jit(solution)/shard_map/all_to_all | solution.py:354
  181.6 25.3 %collective-permute-start.12 = (f32[8,1,16,2048]{3,2,1,0:T(8,128)}, f32[8,1,16,2048]{3,2,1,0:T(8,128)S(1)}, u32[]{:S(2)}, u32[]{:S(2)}) collective-permute-start(f32[8,1,16,2048]{3,2,1,0:T(8,128)} %slice.3), channel_id=1, source_target_pairs={{0,8},{1,9},{2,10},{3,11},{4,12},{5,13},{6,14},{7,15},{8,0},{9,1},... | collective-permute-start | bytes 3145736 | tf_op jit(solution)/shard_map/ppermute | solution.py:358
  (3 other events, 17.1 us)
